TPU v7x, 32 devices: a whole 2x2x4 slice. The times are simulated.
32 devices in a mesh: groups: 2 (over x), dp: 2 (over core), tensor: 8 (over z, y).
Axes of the slice: x: 2, y: 2, z: 4, core: 2. Of those that a mesh axis runs over, the one named last changes fastest.
Arguments:
- hidden: bfloat16 [4, 1024, 8192], P(('groups', 'dp'), 'tensor'), parts along dimension 0, may hold values from -24 to 24
- query_weight: bfloat16 [8192, 4096], P(None, 'tensor'), may hold values from -0.0625 to 0.0625
- key_weight: bfloat16 [8, 4096, 128], P('tensor'), may hold values from -0.0625 to 0.0625
- value_weight: bfloat16 [8, 4096, 128], P('tensor'), may hold values from -0.0625 to 0.0625
- head_grad: bfloat16 [4, 1024, 4096], P(('groups', 'dp'), None, 'tensor'), parts along dimension 0, may hold values from -6 to 6
- lengths: int32 [4], P(('groups', 'dp')), parts along dimension 0, may hold values from 256 to 1024, as said below
Outputs:
- fisher_key: float32 [16, 4096, 128], P(('groups', 'tensor'), 'dp'), parts along dimension 0
- fisher_value: float32 [16, 4096, 128], P(('groups', 'tensor'), 'dp'), parts along dimension 0
There are 2 independent parts, one for each index of `groups`. A program takes and returns all parts, laid end to end along the dimension named above; an argument that names none is the same for every part. Nothing has to cross between parts.
Inputs may be any that keep to these rules, and one draw needn't show every extreme that they name: `lengths`: some sequence of each part has length 1024.
All inputs are finite; a program needn't handle non-finite values.
Results may differ from a plain program's by a relative error of at most 0.013.
The roundings to bfloat16 on the way count: a program that leaves them out, or rounds other values in their place, can miss the bound.
Values may be sent and summed in bfloat16 or wider, within the bound.
A program may use at most 256 MiB of HBM per device.

v0:
```python
import math

import jax
import jax.numpy as jnp
from jax import lax
from jax.sharding import PartitionSpec as P

rope_base = 1000000.0
far_below = -1e30


def from_partner(value, axis, stride):
    mask = 2**stride
    pairs = [(source, source ^ mask) for source in range(lax.axis_size(axis))]
    return lax.ppermute(value, axis, pairs)


def angle_table(length, head_width):
    position = jnp.arange(length, dtype=jnp.float32)[:, None]
    frequency = rope_base ** (-2.0 * jnp.arange(head_width // 2, dtype=jnp.float32) / head_width)
    return (position * frequency)[:, None, :]


def rotate(vectors, angles):
    half_dim = vectors.shape[-1] // 2
    lead_half = vectors[..., :half_dim]
    tail_half = vectors[..., half_dim:]
    cosine = jnp.cos(angles)
    sines = jnp.sin(angles)
    return jnp.concatenate(
        [lead_half * cosine - tail_half * sines, tail_half * cosine + lead_half * sines], axis=-1
    )


def unrotate(vectors, angles):
    half_dim = vectors.shape[-1] // 2
    lead_half = vectors[..., :half_dim]
    tail_half = vectors[..., half_dim:]
    cosine = jnp.cos(angles)
    sines = jnp.sin(angles)
    return jnp.concatenate(
        [lead_half * cosine + tail_half * sines, tail_half * cosine - lead_half * sines], axis=-1
    )


def local(hidden, query_weight, key_weight, value_weight, head_grad, lengths):
    seq_count, tok_rows, model_width = hidden.shape
    length = tok_rows * lax.axis_size("tensor")
    half_width = model_width // 2
    head_width = key_weight.shape[2]
    heads_here = query_weight.shape[1] // head_width
    query_cols = heads_here * head_width
    pair_side = lax.axis_index("tensor") % 2
    score_scale = 1.0 / math.sqrt(head_width)
    angles = angle_table(length, head_width)
    pair_rows = jnp.concatenate([key_weight[0], value_weight[0]], axis=1)
    collected_rows = lax.all_gather(hidden, "tensor", axis=1, tiled=True)
    query_part = jnp.dot(collected_rows, query_weight, preferred_element_type=jnp.float32)
    own_part = lax.dynamic_slice_in_dim(collected_rows, pair_side * half_width, half_width, 2)
    kv_part = jnp.dot(own_part, pair_rows, preferred_element_type=jnp.float32)
    projected = jnp.concatenate([query_part, kv_part], axis=-1)
    kv_mixed = projected[..., query_cols:]
    kv_mixed = kv_mixed + from_partner(kv_mixed, "tensor", 0)
    queries = rotate(
        projected[..., :query_cols].reshape(seq_count, length, heads_here, head_width), angles
    ).astype(jnp.bfloat16)
    keys = rotate(kv_mixed[..., :head_width][:, :, None, :], angles)[:, :, 0, :].astype(
        jnp.bfloat16
    )
    values = kv_mixed[..., head_width:].astype(jnp.bfloat16)
    live_rows = jnp.arange(length, dtype=jnp.int32)[None, :] < lengths[:, None]
    upstream = jnp.where(live_rows[:, :, None], head_grad, jnp.zeros_like(head_grad)).reshape(
        seq_count, length, heads_here, head_width
    )
    block_rows = 512
    block_count = length // block_rows
    kv_accum = jnp.zeros((seq_count, length, 2 * head_width), jnp.float32)
    for block_idx in range(block_count):
        row_begin = block_idx * block_rows
        row_end = row_begin + block_rows
        query_block = queries[:, row_begin:row_end]
        up_block = upstream[:, row_begin:row_end]
        key_tile_block = keys[:, :row_end]
        value_block = values[:, :row_end]
        scores = (
            jnp.einsum(
                "sqhd,skd->shqk", query_block, key_tile_block, preferred_element_type=jnp.float32
            )
            * score_scale
        )
        causal_ok = (row_begin + jnp.arange(block_rows))[:, None] >= jnp.arange(row_end)[None, :]
        scores = jnp.where(causal_ok, scores, far_below)
        exp_scores = jnp.exp(scores - jnp.max(scores, axis=-1, keepdims=True))
        prob_rows = exp_scores / jnp.sum(exp_scores, axis=-1, keepdims=True)
        dprob = jnp.einsum(
            "sqhd,skd->shqk", up_block, value_block, preferred_element_type=jnp.float32
        )
        row_dot = jnp.sum(prob_rows * dprob, axis=-1, keepdims=True)
        dscore = (prob_rows * (dprob - row_dot) * score_scale).astype(jnp.bfloat16)
        key_portion = jnp.einsum(
            "shqk,sqhd->skd", dscore, query_block, preferred_element_type=jnp.float32
        )
        value_part = jnp.einsum(
            "shqk,sqhd->skd",
            prob_rows.astype(jnp.bfloat16),
            up_block,
            preferred_element_type=jnp.float32,
        )
        block_grad = jnp.concatenate([key_portion, value_part], axis=-1)
        kv_accum = kv_accum + jnp.pad(block_grad, ((0, 0), (0, length - row_end), (0, 0)))
    kv_accum = kv_accum + from_partner(kv_accum, "tensor", 0)
    key_gradient = unrotate(kv_accum[..., :head_width][:, :, None, :], angles)[:, :, 0, :]
    key_value_gradient = jnp.concatenate(
        [key_gradient, kv_accum[..., head_width:]], axis=-1
    ).astype(jnp.bfloat16)
    owned_columns = lax.dynamic_slice_in_dim(collected_rows, pair_side * half_width, half_width, 2)
    sample_count = jnp.einsum(
        "jyv,jyo->jvo", owned_columns, key_value_gradient, preferred_element_type=jnp.float32
    )
    squares = jnp.sum(sample_count * sample_count, axis=0)
    fisher_key, fisher_value = (
        lax.psum_scatter(squares[:, :head_width], "dp", scatter_dimension=0, tiled=True),
        lax.psum_scatter(squares[:, head_width:], "dp", scatter_dimension=0, tiled=True),
    )
    return (fisher_key[None], fisher_value[None])


def solution(mesh):
    in_specs = (
        P(("groups", "dp"), "tensor", None),
        P(None, "tensor"),
        P("tensor", None, None),
        P("tensor", None, None),
        P(("groups", "dp"), None, "tensor"),
        P(("groups", "dp")),
    )
    out_specs = (P(("groups", "tensor"), "dp", None), P(("groups", "tensor"), "dp", None))
    return jax.shard_map(local, mesh=mesh, in_specs=in_specs, out_specs=out_specs, check_vma=False)
```

profile of v0, /device:TPU:0, one launch (start us, length us, event | category | flops | bytes accessed | tf_op | source)
XLA Modules:
  0.0 360.1 jit_solution(1559386330099793040)
XLA Ops:
  7.2 0.7 all-gather.2.cloned.1.call-update
  8.0 11.4 %copy.50 = bf16[512,8192]{1,0:T(8,128)(2,1)} copy(bf16[512,8192]{0,1:T(8,128)(2,1)} %bitcast.207) | data formatting | bytes 16777216 | tf_op jit(solution)/shard_map/dot_general | solution.py:58
  19.3 0.5 copy.24
  20.7 1.0 fusion.80
  21.7 0.4 iota_compare_fusion
  22.1 218.3 %all-gather.2.cloned.1.call-done = bf16[1,1024,8192]{2,1,0:T(8,128)(2,1)} async-done(((bf16[1,128,8192]{2,1,0:T(8,128)(2,1)}), bf16[1,1024,8192]{2,1,0:T(8,128)(2,1)}) %all-gather.2.cloned.1.call-update) | async-done | bytes 16777232 | tf_op jit(solution)/shard_map/all_gather | solution.py:57
  240.5 6.3 %fusion.49 = f32[1,1024,256]{1,2,0:T(8,128)S(1)} fusion(bf16[4096,128]{1,0:T(8,128)(2,1)} %bitcast.215, bf16[4096,128]{1,0:T(8,128)(2,1)} %bitcast.216, bf16[1,1024,8192]{2,1,0:T(8,128)(2,1)} %all-gather.2.cloned.1.call-done, s32[]{:T(128)S(6)} %select_n.24), kind=kOutput, calls=%fused_computation.48 | convolution fusion | flops 2151677952 | bytes 11534340 | tf_op jit(solution)/shard_map/dot_general | solution.py:60
  246.8 0.6 collective-permute-start
  247.4 14.4 %fusion.44 = f32[1,1024,4,128]{1,3,2,0:T(8,128)S(1)} fusion(bf16[4,128,8192]{2,1,0:T(8,128)(2,1)} %bitcast.208, bf16[1,1024,8192]{2,1,0:T(8,128)(2,1)} %all-gather.2.cloned.1.call-done), kind=kOutput, calls=%fused_computation.47 | convolution fusion | flops 8589934592 | bytes 27262976 | tf_op jit(solution)/shard_map/dot_general | solution.py:58
  261.8 0.4 add_convert_fusion
  262.1 9.2 %collective-permute-done = f32[1,1024,256]{1,2,0:T(8,128)S(1)} collective-permute-done((f32[1,1024,256]{1,2,0:T(8,128)S(1)}, f32[1,1024,256]{1,2,0:T(8,128)S(1)}, u32[]{:S(2)}, u32[]{:S(2)}) %collective-permute-start) | collective-permute-done | bytes 1048608 | tf_op jit(solution)/shard_map/ppermute | solution.py:15
  271.3 0.2 fusion.102
  271.6 1.2 subtract_convert_fusion.2
  272.8 1.7 fusion.14
  274.5 2.0 fusion.11
  276.5 2.7 fusion.54
  279.3 5.0 %fusion.2 = (f32[4,512]{1,0:T(4,128)S(1)}, f32[1024,512,4]{1,0,2:T(8,128)}) fusion(f32[4,512]{1,0:T(4,128)S(1)} %fusion.11, f32[4,512]{1,0:T(4,128)S(1)} %get-tuple-element.18, f32[1024,512,4]{1,0,2:T(8,128)S(1)} %get-tuple-element.19, pred[512,1024]{0,1:T(8,128)(4,1)S(1)} %iota_compare_fusion, bf16[1,1024,4,128]{1,3,2,0:T(8,128)(2,1)S(1)} %bitcast.210, ...), kind=kOutput, calls=%fused_computation.5 | convolution fusion | flops 549451776 | bytes 18112512 | tf_op jit(solution)/shard_map/sqhd,skd->shqk/dot_general | solution.py:95
  284.3 0.9 fusion.30
  285.2 0.9 fusion.29
  286.1 1.7 fusion.21
  287.8 1.4 fusion.60
  289.2 6.2 %fusion.57 = f32[1,1024,128]{1,2,0:T(8,128)S(1)} fusion(f32[1024,512,4]{1,0,2:T(8,128)} %get-tuple-element.21, f32[4,512]{1,0:T(4,128)S(1)} %get-tuple-element.20, f32[4,512]{1,0:T(4,128)S(1)} %fusion.11, f32[4,512]{1,0:T(4,128)S(1)} %get-tuple-element.18, f32[1024,512,4]{1,0,2:T(8,128)S(1)} %get-tuple-element.19, ...), kind=kOutput, calls=%fused_computation.50 | convolution fusion | flops 554696704 | bytes 18898944 | tf_op jit(solution)/shard_map/shqk,sqhd->skd/dot_general | solution.py:100
  295.4 1.8 fusion.63
  297.4 0.6 collective-permute-start.1
  298.0 23.0 %collective-permute-done.1 = f32[1,1024,256]{1,2,0:T(8,128)S(1)} collective-permute-done((f32[1,1024,256]{1,2,0:T(8,128)S(1)}, f32[1,1024,256]{1,2,0:T(8,128)S(1)}, u32[]{:S(2)}, u32[]{:S(2)}) %collective-permute-start.1) | collective-permute-done | bytes 1048608 | tf_op jit(solution)/shard_map/ppermute | solution.py:15
  321.0 0.2 add.50
  321.3 1.2 add_convert_fusion.1
  322.5 6.0 %fusion.15 = f32[4096,256]{1,0:T(8,128)S(1)} fusion(bf16[1,1024,8192]{2,1,0:T(8,128)(2,1)} %all-gather.2.cloned.1.call-done, s32[]{:T(128)S(6)} %select_n.24, bf16[1024,128]{0,1:T(8,128)(2,1)S(1)} %fusion.75, bf16[1024,128]{0,1:T(8,128)(2,1)S(1)} %maximum_bitcast_fusion.3), kind=kOutput, calls=%fused_computation.19 | convolution fusion | flops 2149580800 | bytes 13107204 | tf_op jit(solution)/shard_map/jyv,jyo->jvo/dot_general | solution.py:117
  328.5 2.2 fusion.103
  330.7 0.7 reduce-scatter.5.cloned.1.call-update
  331.4 8.4 %reduce-scatter.3.cloned.1.call-done = f32[2048,128]{1,0:T(8,128)} async-done(((f32[4096,128]{1,0:T(8,128)}), f32[2048,128]{1,0:T(8,128)}) %reduce-scatter.3.cloned.1.call-update) | async-done | bytes 1048592 | tf_op jit(solution)/shard_map/reduce_scatter | solution.py:122
  339.9 13.7 %reduce-scatter.5.cloned.1.call-done = f32[2048,128]{1,0:T(8,128)} async-done(((f32[4096,128]{1,0:T(8,128)}), f32[2048,128]{1,0:T(8,128)}) %reduce-scatter.5.cloned.1.call-update) | async-done | bytes 1048592 | tf_op jit(solution)/shard_map/reduce_scatter | solution.py:123
  (17 shorter events, 0.6 us)
Async XLA Ops:
  7.2 233.3 %all-gather.2.cloned.1.call-start = ((), (), s32[]{:S(2)}) async-start(), calls=%async_computation.2 | async-start | bytes 18874368 | tf_op jit(solution)/shard_map/all_gather | solution.py:57
  7.9 332.0 %reduce-scatter.3.cloned.1.call-start = ((), (), s32[]{:S(2)}) async-start(), calls=%async_computation.3 | async-start | bytes 3145728 | tf_op jit(solution)/shard_map/reduce_scatter | solution.py:122
  8.0 11.4 %copy-start = (bf16[1,1024,512]{2,1,0:T(8,128)(2,1)S(1)}, bf16[1,1024,512]{2,1,0:T(8,128)(2,1)}, u32[]{:S(2)}) copy-start(bf16[1,1024,512]{2,1,0:T(8,128)(2,1)} %param.10) | copy-start | bytes 3145732
  246.8 24.6 %collective-permute-start = (f32[1,1024,256]{1,2,0:T(8,128)S(1)}, f32[1,1024,256]{1,2,0:T(8,128)S(1)}, u32[]{:S(2)}, u32[]{:S(2)}) collective-permute-start(f32[1,1024,256]{1,2,0:T(8,128)S(1)} %fusion.49), channel_id=1, source_target_pairs={{0,1},{1,0},{2,3},{3,2},{4,5},{5,4},{6,7},{7,6},{8,9},{9,8},{10,11... | collective-permute-start | bytes 3145736 | tf_op jit(solution)/shard_map/ppermute | solution.py:15
  297.4 23.6 %collective-permute-start.1 = (f32[1,1024,256]{1,2,0:T(8,128)S(1)}, f32[1,1024,256]{1,2,0:T(8,128)S(1)}, u32[]{:S(2)}, u32[]{:S(2)}) collective-permute-start(f32[1,1024,256]{1,2,0:T(8,128)S(1)} %fusion.66), channel_id=1, source_target_pairs={{0,1},{1,0},{2,3},{3,2},{4,5},{5,4},{6,7},{7,6},{8,9},{9,8},{10,11... | collective-permute-start | bytes 3145736 | tf_op jit(solution)/shard_map/ppermute | solution.py:15
  330.7 22.9 %reduce-scatter.5.cloned.1.call-start = ((), (), s32[]{:S(2)}) async-start(), calls=%async_computation.4 | async-start | bytes 3145728 | tf_op jit(solution)/shard_map/reduce_scatter | solution.py:123
Sparse Core Ops, SparseCore 0:
  10.1 230.3 all-gather.1
  330.8 9.0 reduce-scatter.2
  342.8 10.7 reduce-scatter.4
where the time goes:
time: 361 us; the launch traced here: 360 us
  waiting for transfers between devices  274 us (76%)
  matrix products  48.1 us (13%)
  between operations  14.6 us (4%)
  local copies, waits for them, and re-layouts  14.2 us (4%)
  other arithmetic  7.71 us (2%)
    all_gather x1, waiting for transfers between devices, local(): collected_rows = lax.all_gather(hidden, 'tensor', axis=1, tiled=True)  218 us
    ppermute x2, waiting for transfers between devices, from_partner(): return lax.ppermute(value, axis, pairs)  32.2 us
    dot_general x1, matrix products, local(): jnp.dot(collected_rows, query_weight, preferred_element_type=jnp.float32)  14.4 us
    reduce_scatter x1, waiting for transfers between devices, local(): lax.psum_scatter(squares[:, head_width:], 'dp', scatter_dimension=0, tile...  13.7 us
    dot_general x1, local copies, waits for them, and re-layouts, local(): jnp.dot(collected_rows, query_weight, preferred_element_type=jnp.float32)  11.4 us
    reduce_scatter x1, waiting for transfers between devices, local(): lax.psum_scatter(squares[:, :head_width], 'dp', scatter_dimension=0, tile...  8.45 us
    dot_general x2, matrix products, local(): jnp.einsum('shqk,sqhd->skd', dscore, query_block, preferred_element_type=...  8.03 us
  transfers between devices with their start and end apart: 5, of which 5 were waited for; matrix products, arithmetic and copies ran while one was open for 8% of the time, Pallas kernels for 0%

commit v1 on v0

--- a/solution.py
+++ b/solution.py
@@ -1,9 +1,14 @@
+import functools
 import math
 
 import jax
 import jax.numpy as jnp
 from jax import lax
+from jax.experimental import pallas as pl
+from jax.experimental.pallas import tpu as pltpu
 from jax.sharding import PartitionSpec as P
+
+MESH = pl.DeviceIdType.MESH
 
 rope_base = 1000000.0
 far_below = -1e30
@@ -43,6 +48,255 @@
     )
 
 
+def gather_project_kernel(
+    count, dp_count, hidden_ref, query_ref, key_ref, value_ref,
+    rows_out, own_out, other_out,
+    held, weights, partial,
+    rows_recv, up_send, down_send, mate_send, load_sem, weight_send, weight_recv,
+    share_send, share_recv, partial_send, partial_recv, rows_store, own_store,
+):
+    me = lax.axis_index("tensor")
+    core = lax.axis_index("dp")
+    side = lax.rem(me, 2)
+    place = lax.div(me, 2)
+    mate = me + 1 - 2 * side
+    chain = count // 2
+    half = held.shape[2]
+    query_cols = query_ref.shape[1]
+    head_width = key_ref.shape[1]
+    own_cols = query_cols + 2 * head_width
+    has_up = place < chain - 1
+    has_down = place > 0
+    share = half // dp_count
+
+    barrier = pltpu.get_barrier_semaphore()
+    pl.semaphore_signal(barrier, inc=1, device_id={"tensor": mate}, device_id_type=MESH)
+    for step in range(1, dp_count):
+        peer = lax.rem(core + step, dp_count)
+        pl.semaphore_signal(barrier, inc=1, device_id={"dp": peer}, device_id_type=MESH)
+
+    @pl.when(has_up)
+    def _():
+        pl.semaphore_signal(barrier, inc=1, device_id={"tensor": me + 2}, device_id_type=MESH)
+
+    @pl.when(has_down)
+    def _():
+        pl.semaphore_signal(barrier, inc=1, device_id={"tensor": me - 2}, device_id_type=MESH)
+
+    edges = jnp.where(has_up, 1, 0) + jnp.where(has_down, 1, 0)
+    pl.semaphore_wait(barrier, dp_count + edges)
+
+    own_half = hidden_ref.at[:, pl.ds(pl.multiple_of(side * half, half), half)]
+    mate_half = hidden_ref.at[:, pl.ds(pl.multiple_of((1 - side) * half, half), half)]
+
+    def up_copy(slot, source):
+        return pltpu.make_async_remote_copy(
+            src_ref=source, dst_ref=held.at[slot], send_sem=up_send.at[slot],
+            recv_sem=rows_recv.at[slot], device_id={"tensor": me + 2}, device_id_type=MESH)
+
+    def down_copy(slot, source):
+        return pltpu.make_async_remote_copy(
+            src_ref=source, dst_ref=held.at[slot], send_sem=down_send.at[slot],
+            recv_sem=rows_recv.at[slot], device_id={"tensor": me - 2}, device_id_type=MESH)
+
+    def wait_rows(slot):
+        pltpu.make_async_remote_copy(
+            src_ref=held.at[slot], dst_ref=held.at[slot], send_sem=mate_send,
+            recv_sem=rows_recv.at[slot], device_id={"tensor": mate}, device_id_type=MESH).wait_recv()
+
+    def store_rows(slot):
+        return pltpu.make_async_copy(held.at[slot], rows_out.at[slot], rows_store.at[slot])
+
+    def store_own(slot):
+        return pltpu.make_async_copy(
+            partial.at[slot, :, pl.ds(0, own_cols)], own_out.at[slot], own_store.at[slot])
+
+    def partial_copy(slot):
+        return pltpu.make_async_remote_copy(
+            src_ref=partial.at[slot, :, pl.ds(query_cols, own_cols)], dst_ref=other_out.at[slot],
+            send_sem=partial_send.at[slot], recv_sem=partial_recv.at[slot],
+            device_id={"tensor": mate}, device_id_type=MESH)
+
+    to_mate = pltpu.make_async_remote_copy(
+        src_ref=mate_half, dst_ref=held.at[me], send_sem=mate_send,
+        recv_sem=rows_recv.at[me], device_id={"tensor": mate}, device_id_type=MESH)
+    to_mate.start()
+
+    @pl.when(has_up)
+    def _():
+        up_copy(me, own_half).start()
+
+    @pl.when(has_down)
+    def _():
+        down_copy(me, own_half).start()
+
+    half_rows = pl.ds(pl.multiple_of(side * half, half), half)
+    loads = [
+        pltpu.make_async_copy(own_half, held.at[me], load_sem.at[0]),
+        pltpu.make_async_copy(
+            query_ref.at[half_rows], weights.at[:, pl.ds(0, query_cols)], load_sem.at[1]),
+        pltpu.make_async_copy(
+            key_ref, weights.at[:, pl.ds(query_cols, head_width)], load_sem.at[2]),
+        pltpu.make_async_copy(
+            value_ref, weights.at[:, pl.ds(query_cols + head_width, head_width)], load_sem.at[3]),
+    ]
+    for load in loads:
+        load.start()
+
+    share_rows = pl.ds(pl.multiple_of(core * share, share), share)
+    mate_cols = pl.ds(own_cols, query_cols)
+    weight_copy = pltpu.make_async_remote_copy(
+        src_ref=query_ref.at[pl.ds(pl.multiple_of((1 - side) * half + core * share, share), share)],
+        dst_ref=weights.at[share_rows, mate_cols], send_sem=weight_send, recv_sem=weight_recv,
+        device_id={"tensor": mate}, device_id_type=MESH)
+
+    wait_rows(mate)
+
+    @pl.when(has_up)
+    def _():
+        up_copy(mate, held.at[mate]).start()
+
+    @pl.when(has_down)
+    def _():
+        down_copy(mate, held.at[mate]).start()
+
+    weight_copy.start()
+
+    def slot_at(step, which):
+        return 2 * step + jnp.where(which == 0, side, 1 - side)
+
+    def receive(distance, which):
+        below = place - distance
+        above = place + distance
+
+        @pl.when(below >= 0)
+        def _():
+            slot = slot_at(below, which)
+            wait_rows(slot)
+
+            @pl.when(has_up)
+            def _():
+                up_copy(slot, held.at[slot]).start()
+
+        @pl.when(above < chain)
+        def _():
+            slot = slot_at(above, which)
+            wait_rows(slot)
+
+            @pl.when(has_down)
+            def _():
+                down_copy(slot, held.at[slot]).start()
+
+    def project(slot):
+        store_rows(slot).start()
+
+        @pl.loop(0, weights.shape[1] // 256)
+        def _(tile):
+            columns = pl.ds(pl.multiple_of(tile * 256, 256), 256)
+            partial[slot, :, columns] = jnp.dot(
+                held[slot], weights[:, columns], preferred_element_type=jnp.float32)
+
+        partial_copy(slot).start()
+        store_own(slot).start()
+
+    def project_at(distance, which):
+        below = place - distance
+        above = place + distance
+
+        @pl.when(below >= 0)
+        def _():
+            project(slot_at(below, which))
+
+        @pl.when(above < chain)
+        def _():
+            project(slot_at(above, which))
+
+    receive(1, 0)
+    receive(1, 1)
+    for load in loads:
+        load.wait()
+    weight_copy.wait_recv()
+    shares = []
+    for step in range(1, dp_count):
+        peer = lax.rem(core + step, dp_count)
+        shares.append(pltpu.make_async_remote_copy(
+            src_ref=weights.at[share_rows, mate_cols], dst_ref=weights.at[share_rows, mate_cols],
+            send_sem=share_send.at[step - 1], recv_sem=share_recv.at[step - 1],
+            device_id={"dp": peer}, device_id_type=MESH))
+    for copy in shares:
+        copy.start()
+    for copy in shares:
+        copy.wait_recv()
+
+    @pl.loop(0, 2)
+    def _(which):
+        project(slot_at(place, which))
+
+    @pl.loop(0, 2)
+    def _(which):
+        project_at(1, which)
+
+    @pl.loop(4, 2 * chain)
+    def _(step):
+        distance = lax.div(step, 2)
+        which = lax.rem(step, 2)
+        receive(distance, which)
+        project_at(distance, which)
+
+    to_mate.wait_send()
+    weight_copy.wait_send()
+    for copy in shares:
+        copy.wait_send()
+
+    @pl.loop(0, count)
+    def _(slot):
+        partial_copy(slot).wait()
+        store_rows(slot).wait()
+        store_own(slot).wait()
+        origin = lax.div(slot, 2)
+
+        @pl.when(has_up & (origin <= place))
+        def _():
+            up_copy(slot, held.at[slot]).wait_send()
+
+        @pl.when(has_down & (origin >= place))
+        def _():
+            down_copy(slot, held.at[slot]).wait_send()
+
+
+def gather_project(hidden, query_weight, key_weight, value_weight):
+    count = lax.axis_size("tensor")
+    dp_count = lax.axis_size("dp")
+    rows, model_width = hidden.shape
+    half = model_width // 2
+    query_cols = query_weight.shape[1]
+    head_width = key_weight.shape[1]
+    own_cols = query_cols + 2 * head_width
+    all_cols = own_cols + query_cols
+    dma = pltpu.SemaphoreType.DMA
+    anywhere = pl.BlockSpec(memory_space=pl.ANY)
+    return pl.pallas_call(
+        functools.partial(gather_project_kernel, count, dp_count),
+        out_shape=(
+            jax.ShapeDtypeStruct((count, rows, half), jnp.bfloat16),
+            jax.ShapeDtypeStruct((count, rows, own_cols), jnp.float32),
+            jax.ShapeDtypeStruct((count, rows, own_cols), jnp.float32),
+        ),
+        in_specs=[anywhere] * 4,
+        out_specs=(anywhere,) * 3,
+        scratch_shapes=[
+            pltpu.VMEM((count, rows, half), jnp.bfloat16),
+            pltpu.VMEM((half, all_cols), jnp.bfloat16),
+            pltpu.VMEM((count, rows, all_cols), jnp.float32),
+            dma((count,)), dma((count,)), dma((count,)), dma, dma((4,)), dma, dma,
+            dma((dp_count - 1,)), dma((dp_count - 1,)), dma((count,)), dma((count,)),
+            dma((count,)), dma((count,)),
+        ],
+        compiler_params=pltpu.CompilerParams(
+            collective_id=0, has_side_effects=True, vmem_limit_bytes=52 * 2**20),
+    )(hidden, query_weight, key_weight, value_weight)
+
+
 def local(hidden, query_weight, key_weight, value_weight, head_grad, lengths):
     seq_count, tok_rows, model_width = hidden.shape
     length = tok_rows * lax.axis_size("tensor")
@@ -50,19 +304,18 @@
     head_width = key_weight.shape[2]
     heads_here = query_weight.shape[1] // head_width
     query_cols = heads_here * head_width
-    pair_side = lax.axis_index("tensor") % 2
     score_scale = 1.0 / math.sqrt(head_width)
     angles = angle_table(length, head_width)
-    pair_rows = jnp.concatenate([key_weight[0], value_weight[0]], axis=1)
-    collected_rows = lax.all_gather(hidden, "tensor", axis=1, tiled=True)
-    query_part = jnp.dot(collected_rows, query_weight, preferred_element_type=jnp.float32)
-    own_part = lax.dynamic_slice_in_dim(collected_rows, pair_side * half_width, half_width, 2)
-    kv_part = jnp.dot(own_part, pair_rows, preferred_element_type=jnp.float32)
-    projected = jnp.concatenate([query_part, kv_part], axis=-1)
-    kv_mixed = projected[..., query_cols:]
-    kv_mixed = kv_mixed + from_partner(kv_mixed, "tensor", 0)
+    half_rows, own_part, other_part = gather_project(
+        hidden[0], query_weight, key_weight[0], value_weight[0]
+    )
+    half_rows = half_rows.reshape(seq_count, length, half_width)
+    own_part = own_part.reshape(seq_count, length, -1)
+    other_part = other_part.reshape(seq_count, length, -1)
+    query_sum = own_part[..., :query_cols] + other_part[..., 2 * head_width :]
+    kv_mixed = own_part[..., query_cols:] + other_part[..., : 2 * head_width]
     queries = rotate(
-        projected[..., :query_cols].reshape(seq_count, length, heads_here, head_width), angles
+        query_sum.reshape(seq_count, length, heads_here, head_width), angles
     ).astype(jnp.bfloat16)
     keys = rotate(kv_mixed[..., :head_width][:, :, None, :], angles)[:, :, 0, :].astype(
         jnp.bfloat16
@@ -113,9 +366,8 @@
     key_value_gradient = jnp.concatenate(
         [key_gradient, kv_accum[..., head_width:]], axis=-1
     ).astype(jnp.bfloat16)
-    owned_columns = lax.dynamic_slice_in_dim(collected_rows, pair_side * half_width, half_width, 2)
     sample_count = jnp.einsum(
-        "jyv,jyo->jvo", owned_columns, key_value_gradient, preferred_element_type=jnp.float32
+        "jyv,jyo->jvo", half_rows, key_value_gradient, preferred_element_type=jnp.float32
     )
     squares = jnp.sum(sample_count * sample_count, axis=0)
     fisher_key, fisher_value = (

time: 361 us -> 275 us (0.76)
  waiting for transfers between devices: 274 us -> 45.1 us
  Pallas kernels: 0 us -> 153 us
  matrix products: 48.1 us -> 23.4 us
  other arithmetic: 7.71 us -> 20.2 us
    all_gather x1 -> x0, waiting for transfers between devices: 218 us -> none  [local(): collected_rows = lax.all_gather(hidden, 'tensor', axis=1, tiled=True)]
    pallas_call x0 -> x1, Pallas kernels: none -> 153 us  [gather_project(): pl.pallas_call(functools.partial(gather_project_kernel, count, dp_count),...]
    dot_general x3 -> x1, matrix products: 26.6 us -> 2.64 us  [local(): jnp.einsum('jyv,jyo->jvo', half_rows, key_value_gradient, preferred_eleme...]
    dot_general x1 -> x0, local copies, waits for them, and re-layouts: 11.4 us -> none  [local(): jnp.dot(collected_rows, query_weight, preferred_element_type=jnp.float32)]
    ppermute x2 -> x1, waiting for transfers between devices: 32.2 us -> 21.6 us  [from_partner(): return lax.ppermute(value, axis, pairs)]
    unnamed x3 -> x19, local copies, waits for them, and re-layouts: 0.53 us -> 8.87 us
    another operation x4 -> x5, other arithmetic: 2.88 us -> 10.1 us
    reduce_scatter x1, waiting for transfers between devices: 8.45 us -> 13.7 us  [local(): lax.psum_scatter(squares[:, :head_width], 'dp', scatter_dimension=0, tile...]
  transfers between devices with their start and end apart: 5 -> 3, of which waited for: 5 -> 3; matrix products, arithmetic and copies ran while one was open for 8% -> 0% of each run, Pallas kernels for 0% -> 0%
where the time goes in v1:
time: 275 us
  Pallas kernels  153 us (56%)
  waiting for transfers between devices  45.1 us (16%)
  matrix products  23.4 us (9%)
  other arithmetic  20.2 us (7%)
  local copies, waits for them, and re-layouts  17.2 us (6%)
  between operations  14.9 us (5%)
    pallas_call x1, Pallas kernels, gather_project(): pl.pallas_call(functools.partial(gather_project_kernel, count, dp_count),...  153 us
    ppermute x1, waiting for transfers between devices, from_partner(): return lax.ppermute(value, axis, pairs)  21.6 us
    reduce_scatter x1, waiting for transfers between devices, local(): lax.psum_scatter(squares[:, :head_width], 'dp', scatter_dimension=0, tile...  13.7 us
    another operation x5, other arithmetic  10.1 us
    reduce_scatter x1, waiting for transfers between devices, local(): lax.psum_scatter(squares[:, head_width:], 'dp', scatter_dimension=0, tile...  9.1 us
    unnamed x19, local copies, waits for them, and re-layouts  8.87 us
    dot_general x2, matrix products, local(): jnp.einsum('shqk,sqhd->skd', dscore, query_block, preferred_element_type=...  7.65 us
    dot_general x2, matrix products, local(): jnp.einsum('sqhd,skd->shqk', up_block, value_block, preferred_element_typ...  6.72 us
  transfers between devices with their start and end apart: 3, of which 3 were waited for; matrix products, arithmetic and copies ran while one was open for 0% of the time, Pallas kernels for 0%

profile of v1, /device:TPU:0, one launch (start us, length us, event | category | flops | bytes accessed | tf_op | source)
XLA Modules:
  0.0 275.0 jit_solution(5921972744752932921)
XLA Ops:
  7.3 1.2 copy-done
  8.6 152.7 %shard_map.77 = (bf16[8,128,4096]{2,1,0:T(8,128)(2,1)}, f32[8,128,768]{2,1,0:T(8,128)}, f32[8,128,768]{2,1,0:T(8,128)}) custom-call(bf16[128,8192]{1,0:T(8,128)(2,1)} %bitcast.194, bf16[8192,512]{1,0:T(8,128)(2,1)} %query_ref.1, bf16[4096,128]{1,0:T(8,128)(2,1)S(1)} %bitcast.186, bf16[4096,128]{1,0:T(8,128)(2,1)} %bitcast.195), custom_call_target="tpu_custom_call" | custom-call | tf_op jit(solution)/shard_map/pallas_call | solution.py:278
  161.2 3.0 %fusion.74 = (bf16[1,1024,256]{2,1,0:T(8,128)(2,1)}, f32[1,1024,256]{2,1,0:T(8,128)}) fusion(f32[1,1024,768]{2,1,0:T(8,128)} %bitcast.190, f32[1,1024,768]{2,1,0:T(8,128)} %bitcast.188), kind=kLoop, calls=%fused_computation.99 | loop fusion | flops 524288 | bytes 3670016 | tf_op jit(solution)/shard_map/convert.11
  164.2 2.0 slice_add_fusion
  167.3 2.3 copy.23
  169.6 2.8 %fusion.52 = (f32[1024,64]{1,0:T(8,128)}, f32[1024,64]{1,0:T(8,128)}) fusion(f32[64]{0:T(128)S(1)} %multiply_power_fusion), kind=kLoop, calls=%fused_computation.67 | loop fusion | flops 65536 | bytes 524544 | tf_op jit(solution)/shard_map/cos | solution.py:33
  172.4 1.1 slice_bitcast_fusion.3
  173.5 1.9 copy.20
  175.3 3.1 %fusion.76 = (f32[1,1024,4,64]{1,3,2,0:T(8,128)}, f32[1,1024,4,64]{1,3,2,0:T(8,128)}) fusion(f32[1,1024,4,128]{1,3,2,0:T(8,128)} %bitcast.187), kind=kLoop, calls=%fused_computation.101 | loop fusion | bytes 4194304 | tf_op jit(solution)/shard_map/slice | solution.py:31
  178.4 2.9 %subtract_convert_fusion.2 = (bf16[1,1024,1,64]{3,1,2,0:T(8,128)(2,1)}, bf16[1,1024,1,64]{3,1,2,0:T(8,128)(2,1)}) fusion(f32[1,1024,1,128]{3,1,2,0:T(8,128)S(1)} %slice_bitcast_fusion.3, f32[64]{0:T(128)S(1)} %multiply_power_fusion), kind=kLoop, calls=%fused_computation.69 | loop fusion | flops 589824 | bytes 786688 | tf_op jit(solution)/shard_map/convert.14
  181.3 1.9 copy.54
  183.2 3.2 %copy.55 = f32[1,1024,4,64]{3,1,2,0:T(8,128)} copy(f32[1,1024,4,64]{1,3,2,0:T(8,128)} %get-tuple-element.15) | data formatting | bytes 2097152
  186.4 1.4 broadcast_select_fusion
  188.3 1.7 add_convert_fusion
  190.4 1.2 fusion.19
  191.5 0.9 fusion.18
  192.5 1.2 fusion.38
  193.7 1.6 fusion.10
  195.3 1.7 fusion.6
  197.0 1.9 fusion.5
  198.9 2.3 fusion.32
  201.2 5.1 %fusion = (f32[4,512]{1,0:T(4,128)S(1)}, f32[1024,512,4]{1,0,2:T(8,128)}) fusion(f32[4,512]{1,0:T(4,128)S(1)} %fusion.5, f32[4,512]{1,0:T(4,128)S(1)} %get-tuple-element.26, f32[1024,512,4]{1,0,2:T(8,128)S(1)} %get-tuple-element.27, pred[512,1024]{0,1:T(8,128)(4,1)S(1)} %iota_compare_fusion, bf16[1,1024,4,128]{1,3,2,0:T(8,128)(2,1)S(1)} %bitcast.199, ...), kind=kOutput, calls=%fused_computation.3 | convolution fusion | flops 549451776 | bytes 18112512 | tf_op jit(solution)/shard_map/sqhd,skd->shqk/dot_general | solution.py:348
  206.3 1.9 fusion.41
  208.2 5.8 %fusion.35 = f32[1,1024,128]{2,1,0:T(8,128)S(1)} fusion(bf16[512,4,128]{2,0,1:T(8,128)(2,1)S(1)} %fusion.47, f32[1024,512,4]{1,0,2:T(8,128)} %get-tuple-element.29, f32[4,512]{1,0:T(4,128)S(1)} %get-tuple-element.28, f32[4,512]{1,0:T(4,128)S(1)} %fusion.5, f32[4,512]{1,0:T(4,128)S(1)} %get-tuple-element.26, f32[1024,512,4]{1,0,2:T(8,128)S(1)} %get-tuple-element.27, ...), kind=kOutput, calls=%fused_computation.40 | convolution fusion | flops 553648128 | bytes 18374656 | tf_op jit(solution)/shard_map/shqk,sqhd->skd/dot_general | solution.py:353
  214.1 1.4 collective-permute-start
  215.5 21.6 %collective-permute-done = f32[1,1024,256]{2,1,0:T(8,128)S(1)} collective-permute-done((f32[1,1024,256]{2,1,0:T(8,128)S(1)}, f32[1,1024,256]{2,1,0:T(8,128)S(1)}, u32[]{:S(2)}, u32[]{:S(2)}) %collective-permute-start) | collective-permute-done | bytes 1048608 | tf_op jit(solution)/shard_map/ppermute | solution.py:20
  237.3 2.2 add_convert_fusion.1
  239.7 2.6 convolution_multiply_fusion
  242.3 2.2 fusion.75
  244.6 0.7 reduce-scatter.3.cloned.1.call-update
  245.3 9.1 %reduce-scatter.5.cloned.1.call-done = f32[2048,128]{1,0:T(8,128)} async-done(((f32[4096,128]{1,0:T(8,128)}), f32[2048,128]{1,0:T(8,128)}) %reduce-scatter.5.cloned.1.call-update) | async-done | bytes 1048592 | tf_op jit(solution)/shard_map/reduce_scatter | solution.py:375
  254.4 13.7 %reduce-scatter.3.cloned.1.call-done = f32[2048,128]{1,0:T(8,128)} async-done(((f32[4096,128]{1,0:T(8,128)}), f32[2048,128]{1,0:T(8,128)}) %reduce-scatter.3.cloned.1.call-update) | async-done | bytes 1048592 | tf_op jit(solution)/shard_map/reduce_scatter | solution.py:374
  (31 shorter events, 1.8 us)
Async XLA Ops:
  7.2 247.3 %reduce-scatter.5.cloned.1.call-start = ((), (), s32[]{:S(2)}) async-start(), calls=%async_computation.3 | async-start | bytes 3145728 | tf_op jit(solution)/shard_map/reduce_scatter | solution.py:375
  7.3 1.2 copy-start
  161.2 3.0 %copy-start.2 = (f32[8,128,768]{2,1,0:T(8,128)S(1)}, f32[8,128,768]{2,1,0:T(8,128)}, u32[]{:S(2)}) copy-start(f32[8,128,768]{2,1,0:T(8,128)} %get-tuple-element.6) | copy-start | bytes 9437188
  181.3 6.5 %copy-start.3 = (bf16[1,1024,1,64]{3,1,2,0:T(8,128)(2,1)S(1)}, bf16[1,1024,1,64]{3,1,2,0:T(8,128)(2,1)}, u32[]{:S(2)}) copy-start(bf16[1,1024,1,64]{3,1,2,0:T(8,128)(2,1)} %get-tuple-element.18) | copy-start | bytes 393220
  181.3 6.6 %copy-start.4 = (bf16[1,1024,1,64]{3,1,2,0:T(8,128)(2,1)S(1)}, bf16[1,1024,1,64]{3,1,2,0:T(8,128)(2,1)}, u32[]{:S(2)}) copy-start(bf16[1,1024,1,64]{3,1,2,0:T(8,128)(2,1)} %get-tuple-element.19) | copy-start | bytes 393220
  186.4 1.9 copy-start.1
  192.5 1.2 copy-start.5
  206.3 33.4 %slice-start = ((s8[8388608]{0:T(1024)(128)(4,1)}), s8[4194304]{0:T(1024)(128)(4,1)S(1)}, s32[]{:S(2)}) async-start(s8[8388608]{0:T(1024)(128)(4,1)} %bitcast.200), calls=%async_computation.4 | async-start | bytes 8388608
  208.2 31.5 %slice-start.1 = ((s8[8388608]{0:T(1024)(128)(4,1)}), s8[4194304]{0:T(1024)(128)(4,1)S(1)}, s32[]{:S(2)}) async-start(s8[8388608]{0:T(1024)(128)(4,1)} %bitcast.200), calls=%async_computation.5 | async-start | bytes 8388608
  214.1 23.0 %collective-permute-start = (f32[1,1024,256]{2,1,0:T(8,128)S(1)}, f32[1,1024,256]{2,1,0:T(8,128)S(1)}, u32[]{:S(2)}, u32[]{:S(2)}) collective-permute-start(f32[1,1024,256]{2,1,0:T(8,128)S(1)} %fusion.44), channel_id=1, source_target_pairs={{0,1},{1,0},{2,3},{3,2},{4,5},{5,4},{6,7},{7,6},{8,9},{9,8},{10,11... | collective-permute-start | bytes 3145736 | tf_op jit(solution)/shard_map/ppermute | solution.py:20
  244.6 23.6 %reduce-scatter.3.cloned.1.call-start = ((), (), s32[]{:S(2)}) async-start(), calls=%async_computation.2 | async-start | bytes 3145728 | tf_op jit(solution)/shard_map/reduce_scatter | solution.py:374
Sparse Core Ops, SparseCore 0:
  244.7 9.6 reduce-scatter.4
  257.3 10.7 reduce-scatter.2

commit v2 on v1

--- a/solution.py
+++ b/solution.py
@@ -14,38 +14,10 @@
 far_below = -1e30
 
 
-def from_partner(value, axis, stride):
-    mask = 2**stride
-    pairs = [(source, source ^ mask) for source in range(lax.axis_size(axis))]
-    return lax.ppermute(value, axis, pairs)
-
-
 def angle_table(length, head_width):
     position = jnp.arange(length, dtype=jnp.float32)[:, None]
     frequency = rope_base ** (-2.0 * jnp.arange(head_width // 2, dtype=jnp.float32) / head_width)
-    return (position * frequency)[:, None, :]
-
-
-def rotate(vectors, angles):
-    half_dim = vectors.shape[-1] // 2
-    lead_half = vectors[..., :half_dim]
-    tail_half = vectors[..., half_dim:]
-    cosine = jnp.cos(angles)
-    sines = jnp.sin(angles)
-    return jnp.concatenate(
-        [lead_half * cosine - tail_half * sines, tail_half * cosine + lead_half * sines], axis=-1
-    )
-
-
-def unrotate(vectors, angles):
-    half_dim = vectors.shape[-1] // 2
-    lead_half = vectors[..., :half_dim]
-    tail_half = vectors[..., half_dim:]
-    cosine = jnp.cos(angles)
-    sines = jnp.sin(angles)
-    return jnp.concatenate(
-        [lead_half * cosine + tail_half * sines, tail_half * cosine - lead_half * sines], axis=-1
-    )
+    return position * frequency
 
 
 def gather_project_kernel(
@@ -296,85 +268,203 @@
             collective_id=0, has_side_effects=True, vmem_limit_bytes=52 * 2**20),
     )(hidden, query_weight, key_weight, value_weight)
 
+def swap_halves(vectors):
+    return pltpu.roll(vectors, vectors.shape[-1] // 2, axis=1)
+
+
+def attend_kernel(
+    dp_count, head_width, lengths_ref, own_ref, other_ref, up_ref, cosine_ref, sine_ref, rows_ref,
+    squares_out, peer_out,
+    queries, keys, values, upstream, rows, grads, mate_grads, rounded, peer_squares,
+    rows_load, grad_send, grad_recv, peer_send, peer_recv,
+):
+    me = lax.axis_index("tensor")
+    core = lax.axis_index("dp")
+    mate = me + 1 - 2 * lax.rem(me, 2)
+    blocks, stacked, _ = queries.shape
+    heads = stacked // head_width
+    step_rows = head_width
+    query_cols = heads * head_width
+    scale = 1.0 / math.sqrt(head_width)
+    share = squares_out.shape[0]
+    tile = 256
+    tiles = share // tile
+
+    barrier = pltpu.get_barrier_semaphore()
+    pl.semaphore_signal(barrier, inc=1, device_id={"tensor": mate}, device_id_type=MESH)
+    for step in range(1, dp_count):
+        peer = lax.rem(core + step, dp_count)
+        pl.semaphore_signal(barrier, inc=1, device_id={"dp": peer}, device_id_type=MESH)
+
+    load = pltpu.make_async_copy(rows_ref, rows, rows_load)
+    load.start()
+    live = lengths_ref[0]
+
+    @pl.loop(0, blocks)
+    def _(block):
+        here = pl.ds(pl.multiple_of(block * step_rows, step_rows), step_rows)
+        cosine = cosine_ref[here, :]
+        sine = sine_ref[here, :]
+        position = block * step_rows + lax.broadcasted_iota(jnp.int32, (step_rows, head_width), 0)
+        alive = position < live
+        for head in range(heads):
+            columns = slice(head * head_width, (head + 1) * head_width)
+            shifted = slice((head + 2) * head_width, (head + 3) * head_width)
+            mixed = own_ref[here, columns] + other_ref[here, shifted]
+            turned = mixed * cosine + swap_halves(mixed) * sine
+            queries[block, columns, :] = turned.astype(jnp.bfloat16)
+            gradient = up_ref[here, columns].astype(jnp.float32)
+            upstream[block, columns, :] = jnp.where(alive, gradient, 0.0).astype(jnp.bfloat16)
+        mixed = own_ref[here, query_cols:query_cols + head_width] + other_ref[here, :head_width]
+        keys[here, :] = (mixed * cosine + swap_halves(mixed) * sine).astype(jnp.bfloat16)
+        values[here, :] = (
+            own_ref[here, query_cols + head_width:] + other_ref[here, head_width:2 * head_width]
+        ).astype(jnp.bfloat16)
+
+    pl.semaphore_wait(barrier, dp_count)
+
+    def grad_copy(block):
+        return pltpu.make_async_remote_copy(
+            src_ref=grads.at[block], dst_ref=mate_grads.at[block],
+            send_sem=grad_send.at[block], recv_sem=grad_recv.at[block],
+            device_id={"tensor": mate}, device_id_type=MESH)
+
+    wide = 2 * head_width
+    contract_last = (((1,), (1,)), ((), ()))
+    for block in reversed(range(blocks)):
+        extent = (block + 1) * step_rows
+        for chunk in range(stacked // wide):
+            chunk_rows = slice(chunk * wide, (chunk + 1) * wide)
+            query = queries[block, chunk_rows, :]
+            above = upstream[block, chunk_rows, :]
+            scores = lax.dot_general(
+                keys[:extent, :], query, contract_last, preferred_element_type=jnp.float32)
+            key_at = lax.broadcasted_iota(jnp.int32, (step_rows, wide), 0)
+            query_at = lax.rem(lax.broadcasted_iota(jnp.int32, (step_rows, wide), 1), step_rows)
+            corner = jnp.where(key_at <= query_at, scores[extent - step_rows:], far_below)
+            if block > 0:
+                scores = jnp.concatenate([scores[:extent - step_rows], corner], axis=0)
+            else:
+                scores = corner
+            peak = jnp.max(scores, axis=0, keepdims=True)
+            powers = jnp.exp((scores - peak) * scale)
+            prob = powers * (1.0 / jnp.sum(powers, axis=0, keepdims=True))
+            dprob = lax.dot_general(
+                values[:extent, :], above, contract_last, preferred_element_type=jnp.float32)
+            row_dot = jnp.sum(prob * dprob, axis=0, keepdims=True)
+            dscore = (prob * (dprob - row_dot) * scale).astype(jnp.bfloat16)
+            key_part = jnp.dot(dscore, query, preferred_element_type=jnp.float32)
+            value_part = jnp.dot(
+                prob.astype(jnp.bfloat16), above, preferred_element_type=jnp.float32)
+            key_part = key_part.reshape(block + 1, step_rows, head_width)
+            value_part = value_part.reshape(block + 1, step_rows, head_width)
+            if block == blocks - 1 and chunk == 0:
+                grads[:, :, :head_width] = key_part
+                grads[:, :, head_width:] = value_part
+            else:
+                grads[:block + 1, :, :head_width] += key_part
+                grads[:block + 1, :, head_width:] += value_part
+        grad_copy(block).start()
+
+    for block in reversed(range(blocks)):
+        here = slice(block * step_rows, (block + 1) * step_rows)
+        grad_copy(block).wait_recv()
+        key_grad = grads[block, :, :head_width] + mate_grads[block, :, :head_width]
+        key_grad = key_grad * cosine_ref[here, :] - swap_halves(key_grad) * sine_ref[here, :]
+        rounded[here, :head_width] = key_grad.astype(jnp.bfloat16)
+        rounded[here, head_width:] = (
+            grads[block, :, head_width:] + mate_grads[block, :, head_width:]
+        ).astype(jnp.bfloat16)
+    load.wait()
+
+    def squares_of(start):
+        columns = pl.ds(pl.multiple_of(start, tile), tile)
+        sample = lax.dot_general(
+            rows[:, columns], rounded[...], (((0,), (0,)), ((), ())),
+            preferred_element_type=jnp.float32)
+        return sample * sample
+
+    def peer_copy(step, index):
+        here = pl.ds(pl.multiple_of(index * tile, tile), tile)
+        return pltpu.make_async_remote_copy(
+            src_ref=peer_squares.at[step - 1, here], dst_ref=peer_out.at[step - 1, here],
+            send_sem=peer_send.at[step - 1, index], recv_sem=peer_recv.at[step - 1, index],
+            device_id={"dp": lax.rem(core + step, dp_count)}, device_id_type=MESH)
+
+    for step in range(1, dp_count):
+        @pl.loop(0, tiles)
+        def _(index):
+            here = pl.ds(pl.multiple_of(index * tile, tile), tile)
+            start = lax.rem(core + step, dp_count) * share + index * tile
+            peer_squares[step - 1, here, :] = squares_of(start)
+            peer_copy(step, index).start()
+
+    @pl.loop(0, tiles)
+    def _(index):
+        here = pl.ds(pl.multiple_of(index * tile, tile), tile)
+        squares_out[here, :] = squares_of(core * share + index * tile)
+
+    for block in range(blocks):
+        grad_copy(block).wait_send()
+    for step in range(1, dp_count):
+        @pl.loop(0, tiles)
+        def _(index):
+            peer_copy(step, index).wait()
+
+
+def attend(lengths, own_part, other_part, head_grad, cosine, sine, half_rows, head_width):
+    dp_count = lax.axis_size("dp")
+    length, half = half_rows.shape
+    heads = head_grad.shape[1] // head_width
+    blocks = length // head_width
+    share = half // dp_count
+    wide = 2 * head_width
+    dma = pltpu.SemaphoreType.DMA
+    here = pl.BlockSpec(memory_space=pltpu.VMEM)
+    anywhere = pl.BlockSpec(memory_space=pl.ANY)
+    return pl.pallas_call(
+        functools.partial(attend_kernel, dp_count, head_width),
+        out_shape=(
+            jax.ShapeDtypeStruct((share, wide), jnp.float32),
+            jax.ShapeDtypeStruct((dp_count - 1, share, wide), jnp.float32),
+        ),
+        in_specs=[pl.BlockSpec(memory_space=pltpu.SMEM)] + [here] * 5 + [anywhere],
+        out_specs=(here, anywhere),
+        scratch_shapes=[
+            pltpu.VMEM((blocks, heads * head_width, head_width), jnp.bfloat16),
+            pltpu.VMEM((length, head_width), jnp.bfloat16),
+            pltpu.VMEM((length, head_width), jnp.bfloat16),
+            pltpu.VMEM((blocks, heads * head_width, head_width), jnp.bfloat16),
+            pltpu.VMEM((length, half), jnp.bfloat16),
+            pltpu.VMEM((blocks, head_width, wide), jnp.float32),
+            pltpu.VMEM((blocks, head_width, wide), jnp.float32),
+            pltpu.VMEM((length, wide), jnp.bfloat16),
+            pltpu.VMEM((dp_count - 1, share, wide), jnp.float32),
+            dma, dma((blocks,)), dma((blocks,)),
+            dma((dp_count - 1, share // 256)), dma((dp_count - 1, share // 256)),
+        ],
+        compiler_params=pltpu.CompilerParams(
+            collective_id=1, has_side_effects=True, vmem_limit_bytes=56 * 2**20),
+    )(lengths, own_part, other_part, head_grad, cosine, sine, half_rows)
+
 
 def local(hidden, query_weight, key_weight, value_weight, head_grad, lengths):
-    seq_count, tok_rows, model_width = hidden.shape
-    length = tok_rows * lax.axis_size("tensor")
-    half_width = model_width // 2
     head_width = key_weight.shape[2]
-    heads_here = query_weight.shape[1] // head_width
-    query_cols = heads_here * head_width
-    score_scale = 1.0 / math.sqrt(head_width)
+    length = head_grad.shape[1]
     angles = angle_table(length, head_width)
+    cosine = jnp.cos(angles)
+    sine = jnp.sin(angles)
+    cosine = jnp.concatenate([cosine, cosine], axis=-1)
+    sine = jnp.concatenate([-sine, sine], axis=-1)
     half_rows, own_part, other_part = gather_project(
         hidden[0], query_weight, key_weight[0], value_weight[0]
     )
-    half_rows = half_rows.reshape(seq_count, length, half_width)
-    own_part = own_part.reshape(seq_count, length, -1)
-    other_part = other_part.reshape(seq_count, length, -1)
-    query_sum = own_part[..., :query_cols] + other_part[..., 2 * head_width :]
-    kv_mixed = own_part[..., query_cols:] + other_part[..., : 2 * head_width]
-    queries = rotate(
-        query_sum.reshape(seq_count, length, heads_here, head_width), angles
-    ).astype(jnp.bfloat16)
-    keys = rotate(kv_mixed[..., :head_width][:, :, None, :], angles)[:, :, 0, :].astype(
-        jnp.bfloat16
+    own_squares, peer_squares = attend(
+        lengths, own_part.reshape(length, -1), other_part.reshape(length, -1), head_grad[0],
+        cosine, sine, half_rows.reshape(length, -1), head_width,
     )
-    values = kv_mixed[..., head_width:].astype(jnp.bfloat16)
-    live_rows = jnp.arange(length, dtype=jnp.int32)[None, :] < lengths[:, None]
-    upstream = jnp.where(live_rows[:, :, None], head_grad, jnp.zeros_like(head_grad)).reshape(
-        seq_count, length, heads_here, head_width
-    )
-    block_rows = 512
-    block_count = length // block_rows
-    kv_accum = jnp.zeros((seq_count, length, 2 * head_width), jnp.float32)
-    for block_idx in range(block_count):
-        row_begin = block_idx * block_rows
-        row_end = row_begin + block_rows
-        query_block = queries[:, row_begin:row_end]
-        up_block = upstream[:, row_begin:row_end]
-        key_tile_block = keys[:, :row_end]
-        value_block = values[:, :row_end]
-        scores = (
-            jnp.einsum(
-                "sqhd,skd->shqk", query_block, key_tile_block, preferred_element_type=jnp.float32
-            )
-            * score_scale
-        )
-        causal_ok = (row_begin + jnp.arange(block_rows))[:, None] >= jnp.arange(row_end)[None, :]
-        scores = jnp.where(causal_ok, scores, far_below)
-        exp_scores = jnp.exp(scores - jnp.max(scores, axis=-1, keepdims=True))
-        prob_rows = exp_scores / jnp.sum(exp_scores, axis=-1, keepdims=True)
-        dprob = jnp.einsum(
-            "sqhd,skd->shqk", up_block, value_block, preferred_element_type=jnp.float32
-        )
-        row_dot = jnp.sum(prob_rows * dprob, axis=-1, keepdims=True)
-        dscore = (prob_rows * (dprob - row_dot) * score_scale).astype(jnp.bfloat16)
-        key_portion = jnp.einsum(
-            "shqk,sqhd->skd", dscore, query_block, preferred_element_type=jnp.float32
-        )
-        value_part = jnp.einsum(
-            "shqk,sqhd->skd",
-            prob_rows.astype(jnp.bfloat16),
-            up_block,
-            preferred_element_type=jnp.float32,
-        )
-        block_grad = jnp.concatenate([key_portion, value_part], axis=-1)
-        kv_accum = kv_accum + jnp.pad(block_grad, ((0, 0), (0, length - row_end), (0, 0)))
-    kv_accum = kv_accum + from_partner(kv_accum, "tensor", 0)
-    key_gradient = unrotate(kv_accum[..., :head_width][:, :, None, :], angles)[:, :, 0, :]
-    key_value_gradient = jnp.concatenate(
-        [key_gradient, kv_accum[..., head_width:]], axis=-1
-    ).astype(jnp.bfloat16)
-    sample_count = jnp.einsum(
-        "jyv,jyo->jvo", half_rows, key_value_gradient, preferred_element_type=jnp.float32
-    )
-    squares = jnp.sum(sample_count * sample_count, axis=0)
-    fisher_key, fisher_value = (
-        lax.psum_scatter(squares[:, :head_width], "dp", scatter_dimension=0, tiled=True),
-        lax.psum_scatter(squares[:, head_width:], "dp", scatter_dimension=0, tiled=True),
-    )
-    return (fisher_key[None], fisher_value[None])
+    squares = own_squares + jnp.sum(peer_squares, axis=0)
+    return (squares[None, :, :head_width], squares[None, :, head_width:])
 
 
 def solution(mesh):

time: 275 us -> 201 us (0.73)
  waiting for transfers between devices: 45.1 us -> 0 us
  Pallas kernels: 153 us -> 192 us
  matrix products: 23.4 us -> 0 us
  local copies, waits for them, and re-layouts: 17.2 us -> 1.46 us
  other arithmetic: 20.2 us -> 5.77 us
  between operations: 14.9 us -> 1.31 us
    pallas_call x0 -> x1, Pallas kernels: none -> 39.2 us  [attend(): pl.pallas_call(functools.partial(attend_kernel, dp_count, head_width), ou...]
    dot_general x9 -> x0, matrix products: 23.4 us -> none  [the longest x2 7.65 us: local(): jnp.einsum('shqk,sqhd->skd', dscore, query_block, preferred_element_type=...]
    reduce_scatter x2 -> x0, waiting for transfers between devices: 22.8 us -> none  [the longest x1 13.7 us: local(): lax.psum_scatter(squares[:, :head_width], 'dp', scatter_dimension=0, tile...]
    ppermute x1 -> x0, waiting for transfers between devices: 21.6 us -> none  [from_partner(): return lax.ppermute(value, axis, pairs)]
    another operation x5 -> x0, other arithmetic: 10.1 us -> none
    unnamed x19 -> x2, local copies, waits for them, and re-layouts: 8.87 us -> 0.01 us
    slice x2 -> x0, local copies, waits for them, and re-layouts: 5.31 us -> none  [the longest x1 3.11 us: rotate(): lead_half = vectors[..., :half_dim]]
    cos x1 -> x0, other arithmetic: 2.83 us -> none  [rotate(): cosine = jnp.cos(angles)]
  transfers between devices with their start and end apart: 3 -> 0, of which waited for: 3 -> 0; matrix products, arithmetic and copies ran while one was open for 0% -> 0% of each run, Pallas kernels for 0% -> 0%
where the time goes in v2:
time: 201 us; the launch traced here: 200 us
  Pallas kernels  192 us (96%)
  other arithmetic  5.77 us (3%)
    pallas_call x1, Pallas kernels, gather_project(): pl.pallas_call(functools.partial(gather_project_kernel, count, dp_count),...  153 us
    pallas_call x1, Pallas kernels, attend(): pl.pallas_call(functools.partial(attend_kernel, dp_count, head_width), ou...  39.2 us

profile of v2, /device:TPU:0, one launch (start us, length us, event | category | flops | bytes accessed | tf_op | source)
XLA Modules:
  0.0 200.4 jit_solution(9718670223727972048)
XLA Ops:
  1.3 0.0 copy-start
  1.3 2.0 fusion.2
  3.3 1.3 pad_maximum_fusion
  4.6 0.0 copy-done
  4.6 152.7 %shard_map.77 = (bf16[8,128,4096]{2,1,0:T(8,128)(2,1)}, f32[8,128,768]{2,1,0:T(8,128)}, f32[8,128,768]{2,1,0:T(8,128)}) custom-call(bf16[128,8192]{1,0:T(8,128)(2,1)} %bitcast.17, bf16[8192,512]{1,0:T(8,128)(2,1)} %query_ref.1, bf16[4096,128]{1,0:T(8,128)(2,1)S(1)} %bitcast.13, bf16[4096,128]{1,0:T(8,128)(2,1)} %bitcast.18), custom_call_target="tpu_custom_call" | custom-call | tf_op jit(solution)/shard_map/pallas_call | solution.py:250
  157.2 39.2 %shard_map.78 = (f32[2048,256]{1,0:T(8,128)}, f32[1,2048,256]{2,1,0:T(8,128)}) custom-call(s32[1]{0:T(128)S(6)} %copy.8.lengths_ref, f32[1024,768]{1,0:T(8,128)} %bitcast.15, f32[1024,768]{1,0:T(8,128)} %bitcast.16, bf16[1024,512]{1,0:T(8,128)(2,1)} %bitcast.19, f32[1024,128]{1,0:T(8,128)} %get-tuple-element.17.cosine_ref, ...), custom_call_target="tpu_custom_call" | custom-call | tf_op jit(solution)/shard_map/pallas_call | solution.py:425
  196.5 2.5 %bitcast_add_fusion = f32[2048,256]{1,0:T(8,128)S(1)} fusion(f32[2048,256]{1,0:T(8,128)} %get-tuple-element.10, f32[1,2048,256]{2,1,0:T(8,128)} %get-tuple-element.11), kind=kLoop, calls=%fused_computation | loop fusion | flops 524288 | bytes 6291456 | tf_op jit(solution)/shard_map/add | solution.py:466
  199.0 1.5 slice_bitcast_fusion
  (1 shorter events, 0.0 us)
Async XLA Ops:
  1.3 3.3 %copy-start = (bf16[1,4096,128]{2,1,0:T(8,128)(2,1)S(1)}, bf16[1,4096,128]{2,1,0:T(8,128)(2,1)}, u32[]{:S(2)}) copy-start(bf16[1,4096,128]{2,1,0:T(8,128)(2,1)} %param.8) | copy-start | bytes 3145732

commit v3 on v2

--- a/solution.py
+++ b/solution.py
@@ -3,6 +3,7 @@
 
 import jax
 import jax.numpy as jnp
+import numpy as np
 from jax import lax
 from jax.experimental import pallas as pl
 from jax.experimental.pallas import tpu as pltpu
@@ -14,18 +15,31 @@
 far_below = -1e30
 
 
-def angle_table(length, head_width):
-    position = jnp.arange(length, dtype=jnp.float32)[:, None]
-    frequency = rope_base ** (-2.0 * jnp.arange(head_width // 2, dtype=jnp.float32) / head_width)
-    return position * frequency
+def turn_table(length, head_width):
+    position = np.arange(length, dtype=np.float64)[:, None]
+    frequency = rope_base ** (-2.0 * np.arange(head_width // 2, dtype=np.float64) / head_width)
+    angles = position * frequency
+    return np.concatenate([np.cos(angles), np.sin(angles)], axis=-1).astype(np.float32)
+
+
+def swap_halves(vectors):
+    return pltpu.roll(vectors, vectors.shape[-1] // 2, axis=1)
+
+
+def cosine_sine(table):
+    other = swap_halves(table)
+    lead = lax.broadcasted_iota(jnp.int32, table.shape, 1) < table.shape[1] // 2
+    return jnp.where(lead, table, other), jnp.where(lead, -other, table)
 
 
 def gather_project_kernel(
-    count, dp_count, hidden_ref, query_ref, key_ref, value_ref,
-    rows_out, own_out, other_out,
-    held, weights, partial,
+    count, dp_count, lengths_ref, gradient_ref, table_ref,
+    hidden_ref, query_ref, key_ref, value_ref,
+    rows_out, queries_out, pairs_out, upstream_out,
+    held, weights, partial, other, queries, pairs, upstream,
     rows_recv, up_send, down_send, mate_send, load_sem, weight_send, weight_recv,
-    share_send, share_recv, partial_send, partial_recv, rows_store, own_store,
+    share_send, share_recv, partial_send, partial_recv, rows_store, queries_store, pairs_store,
+    upstream_store,
 ):
     me = lax.axis_index("tensor")
     core = lax.axis_index("dp")
@@ -79,13 +93,15 @@
     def store_rows(slot):
         return pltpu.make_async_copy(held.at[slot], rows_out.at[slot], rows_store.at[slot])
 
-    def store_own(slot):
-        return pltpu.make_async_copy(
-            partial.at[slot, :, pl.ds(0, own_cols)], own_out.at[slot], own_store.at[slot])
+    def store_queries(slot):
+        return pltpu.make_async_copy(queries.at[slot], queries_out.at[slot], queries_store.at[slot])
+
+    def store_pairs(slot):
+        return pltpu.make_async_copy(pairs.at[slot], pairs_out.at[slot], pairs_store.at[slot])
 
     def partial_copy(slot):
         return pltpu.make_async_remote_copy(
-            src_ref=partial.at[slot, :, pl.ds(query_cols, own_cols)], dst_ref=other_out.at[slot],
+            src_ref=partial.at[slot, :, pl.ds(query_cols, own_cols)], dst_ref=other.at[slot],
             send_sem=partial_send.at[slot], recv_sem=partial_recv.at[slot],
             device_id={"tensor": mate}, device_id_type=MESH)
 
@@ -122,6 +138,21 @@
         dst_ref=weights.at[share_rows, mate_cols], send_sem=weight_send, recv_sem=weight_recv,
         device_id={"tensor": mate}, device_id_type=MESH)
 
+    live = lengths_ref[0]
+    rows = held.shape[1]
+    heads = query_cols // head_width
+
+    @pl.loop(0, count)
+    def _(slot):
+        here = pl.ds(pl.multiple_of(slot * rows, rows), rows)
+        position = slot * rows + lax.broadcasted_iota(jnp.int32, (rows, head_width), 0)
+        for head in range(heads):
+            gradient = gradient_ref[here, head * head_width:(head + 1) * head_width]
+            upstream[slot, head * rows:(head + 1) * rows, :] = jnp.where(
+                position < live, gradient.astype(jnp.float32), 0.0).astype(jnp.bfloat16)
+
+    store_upstream = pltpu.make_async_copy(upstream, upstream_out, upstream_store)
+    store_upstream.start()
     wait_rows(mate)
 
     @pl.when(has_up)
@@ -169,7 +200,6 @@
                 held[slot], weights[:, columns], preferred_element_type=jnp.float32)
 
         partial_copy(slot).start()
-        store_own(slot).start()
 
     def project_at(distance, which):
         below = place - distance
@@ -215,6 +245,43 @@
         receive(distance, which)
         project_at(distance, which)
 
+    def finish(slot):
+        partial_copy(slot).wait_recv()
+        cosine, sine = cosine_sine(table_ref[pl.ds(pl.multiple_of(slot * rows, rows), rows), :])
+
+        def turn(mixed):
+            return (mixed * cosine + swap_halves(mixed) * sine).astype(jnp.bfloat16)
+
+        for head in range(heads):
+            columns = slice(head * head_width, (head + 1) * head_width)
+            shifted = slice((head + 2) * head_width, (head + 3) * head_width)
+            queries[slot, head * rows:(head + 1) * rows, :] = turn(
+                partial[slot, :, columns] + other[slot, :, shifted])
+        pairs[slot, :, :head_width] = turn(
+            partial[slot, :, query_cols:query_cols + head_width] + other[slot, :, :head_width])
+        pairs[slot, :, head_width:] = (
+            partial[slot, :, query_cols + head_width:own_cols]
+            + other[slot, :, head_width:2 * head_width]
+        ).astype(jnp.bfloat16)
+        store_queries(slot).start()
+        store_pairs(slot).start()
+
+    @pl.loop(0, 2 * chain)
+    def _(step):
+        distance = lax.div(step, 2)
+        which = lax.rem(step, 2)
+        below = place - distance
+        above = place + distance
+
+        @pl.when(below >= 0)
+        def _():
+            finish(slot_at(below, which))
+
+        @pl.when((above < chain) & (distance > 0))
+        def _():
+            finish(slot_at(above, which))
+
+    store_upstream.wait()
     to_mate.wait_send()
     weight_copy.wait_send()
     for copy in shares:
@@ -222,9 +289,10 @@
 
     @pl.loop(0, count)
     def _(slot):
-        partial_copy(slot).wait()
+        partial_copy(slot).wait_send()
         store_rows(slot).wait()
-        store_own(slot).wait()
+        store_queries(slot).wait()
+        store_pairs(slot).wait()
         origin = lax.div(slot, 2)
 
         @pl.when(has_up & (origin <= place))
@@ -236,7 +304,7 @@
             down_copy(slot, held.at[slot]).wait_send()
 
 
-def gather_project(hidden, query_weight, key_weight, value_weight):
+def gather_project(lengths, head_grad, table, hidden, query_weight, key_weight, value_weight):
     count = lax.axis_size("tensor")
     dp_count = lax.axis_size("dp")
     rows, model_width = hidden.shape
@@ -245,48 +313,52 @@
     head_width = key_weight.shape[1]
     own_cols = query_cols + 2 * head_width
     all_cols = own_cols + query_cols
+    heads = query_cols // head_width
+    stack_shape = jax.ShapeDtypeStruct((count, heads * rows, head_width), jnp.bfloat16)
+    pair_shape = jax.ShapeDtypeStruct((count, rows, 2 * head_width), jnp.bfloat16)
     dma = pltpu.SemaphoreType.DMA
     anywhere = pl.BlockSpec(memory_space=pl.ANY)
     return pl.pallas_call(
         functools.partial(gather_project_kernel, count, dp_count),
         out_shape=(
             jax.ShapeDtypeStruct((count, rows, half), jnp.bfloat16),
-            jax.ShapeDtypeStruct((count, rows, own_cols), jnp.float32),
-            jax.ShapeDtypeStruct((count, rows, own_cols), jnp.float32),
+            stack_shape,
+            pair_shape,
+            stack_shape,
         ),
-        in_specs=[anywhere] * 4,
-        out_specs=(anywhere,) * 3,
+        in_specs=[pl.BlockSpec(memory_space=pltpu.SMEM)]
+        + [pl.BlockSpec(memory_space=pltpu.VMEM)] * 2 + [anywhere] * 4,
+        out_specs=(anywhere,) * 4,
         scratch_shapes=[
             pltpu.VMEM((count, rows, half), jnp.bfloat16),
             pltpu.VMEM((half, all_cols), jnp.bfloat16),
             pltpu.VMEM((count, rows, all_cols), jnp.float32),
+            pltpu.VMEM((count, rows, own_cols), jnp.float32),
+            pltpu.VMEM(stack_shape.shape, jnp.bfloat16),
+            pltpu.VMEM(pair_shape.shape, jnp.bfloat16),
+            pltpu.VMEM(stack_shape.shape, jnp.bfloat16),
             dma((count,)), dma((count,)), dma((count,)), dma, dma((4,)), dma, dma,
             dma((dp_count - 1,)), dma((dp_count - 1,)), dma((count,)), dma((count,)),
-            dma((count,)), dma((count,)),
+            dma((count,)), dma((count,)), dma((count,)), dma,
         ],
         compiler_params=pltpu.CompilerParams(
-            collective_id=0, has_side_effects=True, vmem_limit_bytes=52 * 2**20),
-    )(hidden, query_weight, key_weight, value_weight)
-
-def swap_halves(vectors):
-    return pltpu.roll(vectors, vectors.shape[-1] // 2, axis=1)
-
+            collective_id=0, has_side_effects=True, vmem_limit_bytes=58 * 2**20),
+    )(lengths, head_grad, table, hidden, query_weight, key_weight, value_weight)
 
 def attend_kernel(
-    dp_count, head_width, lengths_ref, own_ref, other_ref, up_ref, cosine_ref, sine_ref, rows_ref,
+    dp_count, head_width, queries, upstream, pairs, table_ref, rows_ref,
     squares_out, peer_out,
-    queries, keys, values, upstream, rows, grads, mate_grads, rounded, peer_squares,
-    rows_load, grad_send, grad_recv, peer_send, peer_recv,
+    rows, grads, mate_grads, rounded, peer_squares,
+    rows_load, grad_send, grad_recv, final_send, final_recv, peer_send, peer_recv,
 ):
     me = lax.axis_index("tensor")
     core = lax.axis_index("dp")
-    mate = me + 1 - 2 * lax.rem(me, 2)
+    side = lax.rem(me, 2)
+    mate = me + 1 - 2 * side
     blocks, stacked, _ = queries.shape
-    heads = stacked // head_width
     step_rows = head_width
-    query_cols = heads * head_width
     scale = 1.0 / math.sqrt(head_width)
-    share = squares_out.shape[0]
+    share = squares_out.shape[1]
     tile = 256
     tiles = share // tile
 
@@ -298,29 +370,6 @@
 
     load = pltpu.make_async_copy(rows_ref, rows, rows_load)
     load.start()
-    live = lengths_ref[0]
-
-    @pl.loop(0, blocks)
-    def _(block):
-        here = pl.ds(pl.multiple_of(block * step_rows, step_rows), step_rows)
-        cosine = cosine_ref[here, :]
-        sine = sine_ref[here, :]
-        position = block * step_rows + lax.broadcasted_iota(jnp.int32, (step_rows, head_width), 0)
-        alive = position < live
-        for head in range(heads):
-            columns = slice(head * head_width, (head + 1) * head_width)
-            shifted = slice((head + 2) * head_width, (head + 3) * head_width)
-            mixed = own_ref[here, columns] + other_ref[here, shifted]
-            turned = mixed * cosine + swap_halves(mixed) * sine
-            queries[block, columns, :] = turned.astype(jnp.bfloat16)
-            gradient = up_ref[here, columns].astype(jnp.float32)
-            upstream[block, columns, :] = jnp.where(alive, gradient, 0.0).astype(jnp.bfloat16)
-        mixed = own_ref[here, query_cols:query_cols + head_width] + other_ref[here, :head_width]
-        keys[here, :] = (mixed * cosine + swap_halves(mixed) * sine).astype(jnp.bfloat16)
-        values[here, :] = (
-            own_ref[here, query_cols + head_width:] + other_ref[here, head_width:2 * head_width]
-        ).astype(jnp.bfloat16)
-
     pl.semaphore_wait(barrier, dp_count)
 
     def grad_copy(block):
@@ -328,6 +377,30 @@
             src_ref=grads.at[block], dst_ref=mate_grads.at[block],
             send_sem=grad_send.at[block], recv_sem=grad_recv.at[block],
             device_id={"tensor": mate}, device_id_type=MESH)
+
+    def rows_of(block):
+        return slice(block * step_rows, (block + 1) * step_rows)
+
+    def final_copy(block):
+        here = rows_of(block)
+        return pltpu.make_async_remote_copy(
+            src_ref=rounded.at[here], dst_ref=rounded.at[here],
+            send_sem=final_send.at[block], recv_sem=final_recv.at[block],
+            device_id={"tensor": mate}, device_id_type=MESH)
+
+    def finish(block):
+        @pl.when(side == block % 2)
+        def _():
+            grad_copy(block).wait_recv()
+            here = rows_of(block)
+            cosine, sine = cosine_sine(table_ref[here, :])
+            key_grad = grads[block, :, :head_width] + mate_grads[block, :, :head_width]
+            key_grad = key_grad * cosine - swap_halves(key_grad) * sine
+            rounded[here, :head_width] = key_grad.astype(jnp.bfloat16)
+            rounded[here, head_width:] = (
+                grads[block, :, head_width:] + mate_grads[block, :, head_width:]
+            ).astype(jnp.bfloat16)
+            final_copy(block).start()
 
     wide = 2 * head_width
     contract_last = (((1,), (1,)), ((), ()))
@@ -338,7 +411,7 @@
             query = queries[block, chunk_rows, :]
             above = upstream[block, chunk_rows, :]
             scores = lax.dot_general(
-                keys[:extent, :], query, contract_last, preferred_element_type=jnp.float32)
+                pairs[:extent, :head_width], query, contract_last, preferred_element_type=jnp.float32)
             key_at = lax.broadcasted_iota(jnp.int32, (step_rows, wide), 0)
             query_at = lax.rem(lax.broadcasted_iota(jnp.int32, (step_rows, wide), 1), step_rows)
             corner = jnp.where(key_at <= query_at, scores[extent - step_rows:], far_below)
@@ -350,7 +423,7 @@
             powers = jnp.exp((scores - peak) * scale)
             prob = powers * (1.0 / jnp.sum(powers, axis=0, keepdims=True))
             dprob = lax.dot_general(
-                values[:extent, :], above, contract_last, preferred_element_type=jnp.float32)
+                pairs[:extent, head_width:], above, contract_last, preferred_element_type=jnp.float32)
             row_dot = jnp.sum(prob * dprob, axis=0, keepdims=True)
             dscore = (prob * (dprob - row_dot) * scale).astype(jnp.bfloat16)
             key_part = jnp.dot(dscore, query, preferred_element_type=jnp.float32)
@@ -364,17 +437,20 @@
             else:
                 grads[:block + 1, :, :head_width] += key_part
                 grads[:block + 1, :, head_width:] += value_part
-        grad_copy(block).start()
-
+        @pl.when(side != block % 2)
+        def _():
+            grad_copy(block).start()
+
+        if block + 3 < blocks:
+            finish(block + 3)
+
+    for block in reversed(range(min(3, blocks))):
+        finish(block)
     for block in reversed(range(blocks)):
-        here = slice(block * step_rows, (block + 1) * step_rows)
-        grad_copy(block).wait_recv()
-        key_grad = grads[block, :, :head_width] + mate_grads[block, :, :head_width]
-        key_grad = key_grad * cosine_ref[here, :] - swap_halves(key_grad) * sine_ref[here, :]
-        rounded[here, :head_width] = key_grad.astype(jnp.bfloat16)
-        rounded[here, head_width:] = (
-            grads[block, :, head_width:] + mate_grads[block, :, head_width:]
-        ).astype(jnp.bfloat16)
+        @pl.when(side != block % 2)
+        def _():
+            final_copy(block).wait_recv()
+
     load.wait()
 
     def squares_of(start):
@@ -387,7 +463,7 @@
     def peer_copy(step, index):
         here = pl.ds(pl.multiple_of(index * tile, tile), tile)
         return pltpu.make_async_remote_copy(
-            src_ref=peer_squares.at[step - 1, here], dst_ref=peer_out.at[step - 1, here],
+            src_ref=peer_squares.at[step - 1, :, here], dst_ref=peer_out.at[step - 1, :, here],
             send_sem=peer_send.at[step - 1, index], recv_sem=peer_recv.at[step - 1, index],
             device_id={"dp": lax.rem(core + step, dp_count)}, device_id_type=MESH)
 
@@ -396,26 +472,35 @@
         def _(index):
             here = pl.ds(pl.multiple_of(index * tile, tile), tile)
             start = lax.rem(core + step, dp_count) * share + index * tile
-            peer_squares[step - 1, here, :] = squares_of(start)
+            squares = squares_of(start)
+            peer_squares[step - 1, 0, here, :] = squares[:, :head_width]
+            peer_squares[step - 1, 1, here, :] = squares[:, head_width:]
             peer_copy(step, index).start()
 
     @pl.loop(0, tiles)
     def _(index):
         here = pl.ds(pl.multiple_of(index * tile, tile), tile)
-        squares_out[here, :] = squares_of(core * share + index * tile)
+        squares = squares_of(core * share + index * tile)
+        squares_out[0, here, :] = squares[:, :head_width]
+        squares_out[1, here, :] = squares[:, head_width:]
 
     for block in range(blocks):
-        grad_copy(block).wait_send()
+        @pl.when(side != block % 2)
+        def _():
+            grad_copy(block).wait_send()
+
+        @pl.when(side == block % 2)
+        def _():
+            final_copy(block).wait_send()
     for step in range(1, dp_count):
         @pl.loop(0, tiles)
         def _(index):
             peer_copy(step, index).wait()
 
 
-def attend(lengths, own_part, other_part, head_grad, cosine, sine, half_rows, head_width):
+def attend(queries, upstream, pairs, table, half_rows, head_width):
     dp_count = lax.axis_size("dp")
     length, half = half_rows.shape
-    heads = head_grad.shape[1] // head_width
     blocks = length // head_width
     share = half // dp_count
     wide = 2 * head_width
@@ -425,46 +510,39 @@
     return pl.pallas_call(
         functools.partial(attend_kernel, dp_count, head_width),
         out_shape=(
-            jax.ShapeDtypeStruct((share, wide), jnp.float32),
-            jax.ShapeDtypeStruct((dp_count - 1, share, wide), jnp.float32),
+            jax.ShapeDtypeStruct((2, share, head_width), jnp.float32),
+            jax.ShapeDtypeStruct((dp_count - 1, 2, share, head_width), jnp.float32),
         ),
-        in_specs=[pl.BlockSpec(memory_space=pltpu.SMEM)] + [here] * 5 + [anywhere],
+        in_specs=[here] * 4 + [anywhere],
         out_specs=(here, anywhere),
         scratch_shapes=[
-            pltpu.VMEM((blocks, heads * head_width, head_width), jnp.bfloat16),
-            pltpu.VMEM((length, head_width), jnp.bfloat16),
-            pltpu.VMEM((length, head_width), jnp.bfloat16),
-            pltpu.VMEM((blocks, heads * head_width, head_width), jnp.bfloat16),
             pltpu.VMEM((length, half), jnp.bfloat16),
             pltpu.VMEM((blocks, head_width, wide), jnp.float32),
             pltpu.VMEM((blocks, head_width, wide), jnp.float32),
             pltpu.VMEM((length, wide), jnp.bfloat16),
-            pltpu.VMEM((dp_count - 1, share, wide), jnp.float32),
-            dma, dma((blocks,)), dma((blocks,)),
+            pltpu.VMEM((dp_count - 1, 2, share, head_width), jnp.float32),
+            dma, dma((blocks,)), dma((blocks,)), dma((blocks,)), dma((blocks,)),
             dma((dp_count - 1, share // 256)), dma((dp_count - 1, share // 256)),
         ],
         compiler_params=pltpu.CompilerParams(
             collective_id=1, has_side_effects=True, vmem_limit_bytes=56 * 2**20),
-    )(lengths, own_part, other_part, head_grad, cosine, sine, half_rows)
+    )(queries, upstream, pairs, table, half_rows)
 
 
 def local(hidden, query_weight, key_weight, value_weight, head_grad, lengths):
     head_width = key_weight.shape[2]
     length = head_grad.shape[1]
-    angles = angle_table(length, head_width)
-    cosine = jnp.cos(angles)
-    sine = jnp.sin(angles)
-    cosine = jnp.concatenate([cosine, cosine], axis=-1)
-    sine = jnp.concatenate([-sine, sine], axis=-1)
-    half_rows, own_part, other_part = gather_project(
-        hidden[0], query_weight, key_weight[0], value_weight[0]
+    table = jnp.asarray(turn_table(length, head_width))
+    half_rows, queries, pairs, upstream = gather_project(
+        lengths, head_grad[0], table, hidden[0], query_weight, key_weight[0], value_weight[0]
     )
-    own_squares, peer_squares = attend(
-        lengths, own_part.reshape(length, -1), other_part.reshape(length, -1), head_grad[0],
-        cosine, sine, half_rows.reshape(length, -1), head_width,
+    own, peer = attend(
+        queries, upstream, pairs.reshape(length, -1), table, half_rows.reshape(length, -1),
+        head_width,
     )
-    squares = own_squares + jnp.sum(peer_squares, axis=0)
-    return (squares[None, :, :head_width], squares[None, :, head_width:])
+    fisher_key = own[:1] + jnp.sum(peer[:, :1], axis=0)
+    fisher_value = own[1:] + jnp.sum(peer[:, 1:], axis=0)
+    return (fisher_key, fisher_value)
 
 
 def solution(mesh):

time: 201 us -> 195 us (0.970)
  other arithmetic: 5.77 us -> 3.7 us
    pallas_call x1, Pallas kernels: 39.2 us -> 35.2 us  [attend(): pl.pallas_call(functools.partial(attend_kernel, dp_count, head_width), ou...]
    pallas_call x1, Pallas kernels: 153 us -> 155 us  [gather_project(): pl.pallas_call(functools.partial(gather_project_kernel, count, dp_count),...]
where the time goes in v3:
time: 195 us
  Pallas kernels  190 us (97%)
  other arithmetic  3.7 us (2%)
    pallas_call x1, Pallas kernels, gather_project(): pl.pallas_call(functools.partial(gather_project_kernel, count, dp_count),...  155 us
    pallas_call x1, Pallas kernels, attend(): pl.pallas_call(functools.partial(attend_kernel, dp_count, head_width), ou...  35.2 us

profile of v3, /device:TPU:0, one launch (start us, length us, event | category | flops | bytes accessed | tf_op | source)
XLA Modules:
  0.0 195.0 jit_solution(8875886436353824347)
XLA Ops:
  1.3 154.8 %shard_map.86 = (bf16[8,128,4096]{2,1,0:T(8,128)(2,1)}, bf16[8,512,128]{2,1,0:T(8,128)(2,1)}, bf16[8,128,256]{2,1,0:T(8,128)(2,1)}, bf16[8,512,128]{2,1,0:T(8,128)(2,1)}) custom-call(s32[1]{0:T(128)S(6)} %copy.9.lengths_ref, bf16[1024,512]{1,0:T(8,128)(2,1)} %bitcast.12, f32[1024,128]{1,0:T(8,128)} %constant.1.clone.table_ref, bf16[128,8192]{1,0:T(8,128)(2,1)} %bitcast.11, ...), custom_call_target="tpu_custom_call" | custom-call | tf_op jit(solution)/shard_map/pallas_call | solution.py:321
  156.1 35.2 %shard_map.87 = (f32[2,2048,128]{2,1,0:T(8,128)}, f32[1,2,2048,128]{3,2,1,0:T(8,128)}) custom-call(bf16[8,512,128]{2,1,0:T(8,128)(2,1)} %get-tuple-element.8.queries, bf16[8,512,128]{2,1,0:T(8,128)(2,1)} %get-tuple-element.9.upstream, bf16[1024,256]{1,0:T(8,128)(2,1)} %bitcast.15, f32[1024,128]{1,0:T(8,128)} %constant.1.clone.table_ref, ...), custom_call_target="tpu_custom_call" | custom-call | tf_op jit(solution)/shard_map/pallas_call | solution.py:510
  191.3 3.7 %bitcast_add_fusion = (f32[1,2048,128]{2,1,0:T(8,128)}, f32[1,2048,128]{2,1,0:T(8,128)}) fusion(f32[1,2,2048,128]{3,2,1,0:T(8,128)} %get-tuple-element.13, f32[2,2048,128]{2,1,0:T(8,128)} %get-tuple-element.12), kind=kLoop, calls=%fused_computation | loop fusion | flops 524288 | bytes 6291456 | tf_op jit(solution)/shard_map/add | solution.py:544

commit v4 on v3

--- a/solution.py
+++ b/solution.py
@@ -99,10 +99,15 @@
     def store_pairs(slot):
         return pltpu.make_async_copy(pairs.at[slot], pairs_out.at[slot], pairs_store.at[slot])
 
-    def partial_copy(slot):
+    tile = 256
+    pieces = own_cols // tile
+
+    def partial_copy(slot, piece):
+        source = pl.ds(pl.multiple_of(query_cols + piece * tile, tile), tile)
+        target = pl.ds(pl.multiple_of(piece * tile, tile), tile)
         return pltpu.make_async_remote_copy(
-            src_ref=partial.at[slot, :, pl.ds(query_cols, own_cols)], dst_ref=other.at[slot],
-            send_sem=partial_send.at[slot], recv_sem=partial_recv.at[slot],
+            src_ref=partial.at[slot, :, source], dst_ref=other.at[slot, :, target],
+            send_sem=partial_send.at[slot, piece], recv_sem=partial_recv.at[slot, piece],
             device_id={"tensor": mate}, device_id_type=MESH)
 
     to_mate = pltpu.make_async_remote_copy(
@@ -193,13 +198,19 @@
     def project(slot):
         store_rows(slot).start()
 
-        @pl.loop(0, weights.shape[1] // 256)
-        def _(tile):
-            columns = pl.ds(pl.multiple_of(tile * 256, 256), 256)
+        def multiply(start):
+            columns = pl.ds(pl.multiple_of(start, tile), tile)
             partial[slot, :, columns] = jnp.dot(
                 held[slot], weights[:, columns], preferred_element_type=jnp.float32)
 
-        partial_copy(slot).start()
+        @pl.loop(0, pieces)
+        def _(piece):
+            multiply(query_cols + piece * tile)
+            partial_copy(slot, piece).start()
+
+        @pl.loop(0, query_cols // tile)
+        def _(piece):
+            multiply(piece * tile)
 
     def project_at(distance, which):
         below = place - distance
@@ -246,7 +257,8 @@
         project_at(distance, which)
 
     def finish(slot):
-        partial_copy(slot).wait_recv()
+        for piece in range(pieces):
+            partial_copy(slot, piece).wait_recv()
         cosine, sine = cosine_sine(table_ref[pl.ds(pl.multiple_of(slot * rows, rows), rows), :])
 
         def turn(mixed):
@@ -289,7 +301,8 @@
 
     @pl.loop(0, count)
     def _(slot):
-        partial_copy(slot).wait_send()
+        for piece in range(pieces):
+            partial_copy(slot, piece).wait_send()
         store_rows(slot).wait()
         store_queries(slot).wait()
         store_pairs(slot).wait()
@@ -338,7 +351,8 @@
             pltpu.VMEM(pair_shape.shape, jnp.bfloat16),
             pltpu.VMEM(stack_shape.shape, jnp.bfloat16),
             dma((count,)), dma((count,)), dma((count,)), dma, dma((4,)), dma, dma,
-            dma((dp_count - 1,)), dma((dp_count - 1,)), dma((count,)), dma((count,)),
+            dma((dp_count - 1,)), dma((dp_count - 1,)),
+            dma((count, own_cols // 256)), dma((count, own_cols // 256)),
             dma((count,)), dma((count,)), dma((count,)), dma,
         ],
         compiler_params=pltpu.CompilerParams(
@@ -420,7 +434,7 @@
             else:
                 scores = corner
             peak = jnp.max(scores, axis=0, keepdims=True)
-            powers = jnp.exp((scores - peak) * scale)
+            powers = jnp.exp2((scores - peak) * (scale * math.log2(math.e)))
             prob = powers * (1.0 / jnp.sum(powers, axis=0, keepdims=True))
             dprob = lax.dot_general(
                 pairs[:extent, head_width:], above, contract_last, preferred_element_type=jnp.float32)

time: 195 us -> 193 us (0.990)
  Pallas kernels: 190 us -> 188 us
where the time goes in v4:
time: 193 us
  Pallas kernels  188 us (97%)
  other arithmetic  3.7 us (2%)
    pallas_call x1, Pallas kernels, gather_project(): pl.pallas_call(functools.partial(gather_project_kernel, count, dp_count),...  153 us
    pallas_call x1, Pallas kernels, attend(): pl.pallas_call(functools.partial(attend_kernel, dp_count, head_width), ou...  35 us

profile of v4, /device:TPU:0, one launch (start us, length us, event | category | flops | bytes accessed | tf_op | source)
XLA Modules:
  0.0 193.3 jit_solution(17273782335207417793)
XLA Ops:
  1.3 153.3 %shard_map.86 = (bf16[8,128,4096]{2,1,0:T(8,128)(2,1)}, bf16[8,512,128]{2,1,0:T(8,128)(2,1)}, bf16[8,128,256]{2,1,0:T(8,128)(2,1)}, bf16[8,512,128]{2,1,0:T(8,128)(2,1)}) custom-call(s32[1]{0:T(128)S(6)} %copy.9.lengths_ref, bf16[1024,512]{1,0:T(8,128)(2,1)} %bitcast.12, f32[1024,128]{1,0:T(8,128)} %constant.1.clone.table_ref, bf16[128,8192]{1,0:T(8,128)(2,1)} %bitcast.11, ...), custom_call_target="tpu_custom_call" | custom-call | tf_op jit(solution)/shard_map/pallas_call | solution.py:334
  154.6 35.0 %shard_map.87 = (f32[2,2048,128]{2,1,0:T(8,128)}, f32[1,2,2048,128]{3,2,1,0:T(8,128)}) custom-call(bf16[8,512,128]{2,1,0:T(8,128)(2,1)} %get-tuple-element.8.queries, bf16[8,512,128]{2,1,0:T(8,128)(2,1)} %get-tuple-element.9.upstream, bf16[1024,256]{1,0:T(8,128)(2,1)} %bitcast.15, f32[1024,128]{1,0:T(8,128)} %constant.1.clone.table_ref, ...), custom_call_target="tpu_custom_call" | custom-call | tf_op jit(solution)/shard_map/pallas_call | solution.py:524
  189.6 3.7 %bitcast_add_fusion = (f32[1,2048,128]{2,1,0:T(8,128)}, f32[1,2048,128]{2,1,0:T(8,128)}) fusion(f32[1,2,2048,128]{3,2,1,0:T(8,128)} %get-tuple-element.13, f32[2,2048,128]{2,1,0:T(8,128)} %get-tuple-element.12), kind=kLoop, calls=%fused_computation | loop fusion | flops 524288 | bytes 6291456 | tf_op jit(solution)/shard_map/add | solution.py:558

commit v5 on v4

--- a/solution.py
+++ b/solution.py
@@ -195,39 +195,60 @@
             def _():
                 down_copy(slot, held.at[slot]).start()
 
-    def project(slot):
+    def multiply(slot, start):
+        columns = pl.ds(pl.multiple_of(start, tile), tile)
+        partial[slot, :, columns] = jnp.dot(
+            held[slot], weights[:, columns], preferred_element_type=jnp.float32)
+
+    def project_pair(slot):
         store_rows(slot).start()
-
-        def multiply(start):
-            columns = pl.ds(pl.multiple_of(start, tile), tile)
-            partial[slot, :, columns] = jnp.dot(
-                held[slot], weights[:, columns], preferred_element_type=jnp.float32)
-
-        @pl.loop(0, pieces)
+        multiply(slot, query_cols)
+
+    def send_pair(slot):
+        partial_copy(slot, 0).start()
+
+    def project_queries(slot):
+        @pl.loop(1, pieces)
         def _(piece):
-            multiply(query_cols + piece * tile)
+            multiply(slot, query_cols + piece * tile)
             partial_copy(slot, piece).start()
 
         @pl.loop(0, query_cols // tile)
         def _(piece):
-            multiply(piece * tile)
-
-    def project_at(distance, which):
+            multiply(slot, piece * tile)
+
+    def project(slot):
+        project_pair(slot)
+        send_pair(slot)
+        project_queries(slot)
+
+    def project_at(distance, which, action):
         below = place - distance
         above = place + distance
 
         @pl.when(below >= 0)
         def _():
-            project(slot_at(below, which))
+            action(slot_at(below, which))
 
         @pl.when(above < chain)
         def _():
-            project(slot_at(above, which))
+            action(slot_at(above, which))
 
     receive(1, 0)
     receive(1, 1)
     for load in loads:
         load.wait()
+
+    def early(action):
+        @pl.loop(0, 2)
+        def _(which):
+            action(slot_at(place, which))
+
+        @pl.loop(0, 2)
+        def _(which):
+            project_at(1, which, action)
+
+    early(project_pair)
     weight_copy.wait_recv()
     shares = []
     for step in range(1, dp_count):
@@ -238,23 +259,17 @@
             device_id={"dp": peer}, device_id_type=MESH))
     for copy in shares:
         copy.start()
+    early(send_pair)
     for copy in shares:
         copy.wait_recv()
-
-    @pl.loop(0, 2)
-    def _(which):
-        project(slot_at(place, which))
-
-    @pl.loop(0, 2)
-    def _(which):
-        project_at(1, which)
+    early(project_queries)
 
     @pl.loop(4, 2 * chain)
     def _(step):
         distance = lax.div(step, 2)
         which = lax.rem(step, 2)
         receive(distance, which)
-        project_at(distance, which)
+        project_at(distance, which, project)
 
     def finish(slot):
         for piece in range(pieces):

time: 193 us -> 193 us (level)
  no operation moved by 1% of the time
where the time goes in v5:
time: 193 us
  Pallas kernels  188 us (97%)
  other arithmetic  3.7 us (2%)
    pallas_call x1, Pallas kernels, gather_project(): pl.pallas_call(functools.partial(gather_project_kernel, count, dp_count),...  153 us
    pallas_call x1, Pallas kernels, attend(): pl.pallas_call(functools.partial(attend_kernel, dp_count, head_width), ou...  35 us

profile of v5, /device:TPU:0, one launch (start us, length us, event | category | flops | bytes accessed | tf_op | source)
XLA Modules:
  0.0 193.2 jit_solution(2951851815020177866)
XLA Ops:
  1.3 153.3 %shard_map.86 = (bf16[8,128,4096]{2,1,0:T(8,128)(2,1)}, bf16[8,512,128]{2,1,0:T(8,128)(2,1)}, bf16[8,128,256]{2,1,0:T(8,128)(2,1)}, bf16[8,512,128]{2,1,0:T(8,128)(2,1)}) custom-call(s32[1]{0:T(128)S(6)} %copy.9.lengths_ref, bf16[1024,512]{1,0:T(8,128)(2,1)} %bitcast.12, f32[1024,128]{1,0:T(8,128)} %constant.1.clone.table_ref, bf16[128,8192]{1,0:T(8,128)(2,1)} %bitcast.11, ...), custom_call_target="tpu_custom_call" | custom-call | tf_op jit(solution)/shard_map/pallas_call | solution.py:349
  154.6 35.0 %shard_map.87 = (f32[2,2048,128]{2,1,0:T(8,128)}, f32[1,2,2048,128]{3,2,1,0:T(8,128)}) custom-call(bf16[8,512,128]{2,1,0:T(8,128)(2,1)} %get-tuple-element.8.queries, bf16[8,512,128]{2,1,0:T(8,128)(2,1)} %get-tuple-element.9.upstream, bf16[1024,256]{1,0:T(8,128)(2,1)} %bitcast.15, f32[1024,128]{1,0:T(8,128)} %constant.1.clone.table_ref, ...), custom_call_target="tpu_custom_call" | custom-call | tf_op jit(solution)/shard_map/pallas_call | solution.py:539
  189.5 3.7 %bitcast_add_fusion = (f32[1,2048,128]{2,1,0:T(8,128)}, f32[1,2048,128]{2,1,0:T(8,128)}) fusion(f32[1,2,2048,128]{3,2,1,0:T(8,128)} %get-tuple-element.13, f32[2,2048,128]{2,1,0:T(8,128)} %get-tuple-element.12), kind=kLoop, calls=%fused_computation | loop fusion | flops 524288 | bytes 6291456 | tf_op jit(solution)/shard_map/add | solution.py:573
